TPU v7x, 32 devices: a whole 2x2x4 slice. The times are simulated.
32 devices in a mesh: wave: 4 (over y, core), lev: 8 (over z, x).
Axes of the slice: x: 2, y: 2, z: 4, core: 2. Of those that a mesh axis runs over, the one named last changes fastest.
Arguments:
- spectral: bfloat16 [8, 6, 1280, 1280], P('lev', None, 'wave'), may hold values from -0.16992188 to 0.16992188
- legendre: bfloat16 [1280, 6, 1280], P('wave'), may hold values from -0.15625 to 0.15625
- slot_wave: int32 [1280], replicated, may hold values from 0 to 1279, each once
- cycle_len: int32 [6], replicated, may hold values from 2576 to 5136, as said below
- lat_order: int32 [12], replicated, may hold values from 0 to 11, each once
Outputs:
- grid: float32 [12, 124416], P('wave', 'lev')
Inputs may be any that keep to these rules, and one draw needn't show every extreme that they name: `slot_wave`: each wavenumber is held in exactly one slot. `lat_order`: each latitude is held in exactly one row. `cycle_len`: every cycle length is a multiple of 16; some pair has exactly 5136 points and some pair exactly 2576.
All inputs are finite; a program needn't handle non-finite values.
Results may differ from a plain program's by a relative error of at most 0.0003.
Values sent between devices are 32-bit elements; how exact they have to be, the bound alone decides.
A program may use at most 64 MiB of HBM per device.

v0:
```python
import functools
import math

import jax
import jax.numpy as jnp
from jax import lax
from jax.experimental import pallas as pl
from jax.experimental.pallas import tpu as pltpu
from jax.sharding import PartitionSpec as P

RMAX = 5136
FIELDS = 3


def split(value):
    high = value.astype(jnp.bfloat16)
    return high, (value - high.astype(jnp.float32)).astype(jnp.bfloat16)


def dot_nt(left, right):
    return lax.dot_general(left, right, (((1,), (1,)), ((), ())), preferred_element_type=jnp.float32)


def turns(t):
    y = math.pi * t
    z = y * y
    sine = jnp.full_like(z, 1.0 / math.factorial(13))
    for n in (11, 9, 7, 5, 3, 1):
        sign = -1.0 if (n // 2) % 2 else 1.0
        sine = sine * z + sign / math.factorial(n)
    sine = sine * y
    cosine = jnp.full_like(z, 1.0 / math.factorial(12))
    for n in (10, 8, 6, 4, 2, 0):
        sign = -1.0 if (n // 2) % 2 else 1.0
        cosine = cosine * z + sign / math.factorial(n)
    return 1.0 - 2.0 * sine * sine, 2.0 * sine * cosine


def points_kernel(
    step, step_pad, wave_ref, lat_ref, cycle_ref, coef_ref, out_ref,
    e_ref, w_ref, t_ref, place_ref, send_ref, got_ref, own_sem, send_sem, recv_sem,
):
    cycles, lev_count, rows_dev, wide = send_ref.shape
    parts, slots = coef_ref.shape[1:]
    fields = parts // 2
    half_cycles = cycle_ref.shape[0]
    me = lax.axis_index("lev")
    first_row = lax.axis_index("wave") * cycles
    barrier = pltpu.get_barrier_semaphore()
    for offset in range(1, lev_count):
        peer = lax.rem(me + offset, lev_count)
        pl.semaphore_signal(barrier, inc=1, device_id={"lev": peer}, device_id_type=pl.DeviceIdType.MESH)

    waves = wave_ref[...].astype(jnp.float32)
    weights = jnp.where(waves == 0.0, 1.0, 2.0)
    steps_e = (step_pad // 8 + 7) // 8 * 8
    steps_t = (lev_count + 7) // 8 * 8
    at_t = 8 + steps_e
    at_d = at_t + 8
    index = lax.broadcasted_iota(jnp.int32, (at_d + steps_t, 1), 0)
    mult = jnp.where(
        index < 8,
        index,
        jnp.where(index < at_t, 8 * (index - 8), jnp.where(index < at_d, step * (index - at_t), 8 * step * (index - at_d))),
    ).astype(jnp.float32)
    products = waves * mult
    copies = []
    for r in range(cycles):
        length = cycle_ref[lat_ref[first_row + r] % half_cycles].astype(jnp.float32)
        inverse = 1.0 / jnp.full((1, slots), length)
        whole = jnp.floor(products * inverse + 0.5)
        cosine, sine = turns((products - whole * length) * inverse)
        for k in range(step_pad // 8):
            c0, s0, c1, s1 = cosine[0:8], sine[0:8], cosine[8 + k : 9 + k], sine[8 + k : 9 + k]
            e_ref[0, 8 * k : 8 * k + 8] = c0 * c1 - s0 * s1
            e_ref[1, 8 * k : 8 * k + 8] = s0 * c1 + c0 * s1
        for k in range((lev_count + 1) // 2):
            tc, ts = [], []
            for d in (2 * k, 2 * k + 1):
                c0, s0 = cosine[at_t : at_d], sine[at_t : at_d]
                c1, s1 = cosine[at_d + d : at_d + d + 1], sine[at_d + d : at_d + d + 1]
                tc.append(c0 * c1 - s0 * s1)
                ts.append(s0 * c1 + c0 * s1)
            for place, value in ((0, tc), (slots, ts)):
                high, low = split(jnp.concatenate(value, axis=0))
                t_ref[0, 16 * k : 16 * k + 16, place : place + slots] = high
                t_ref[1, 16 * k : 16 * k + 16, place : place + slots] = low
        for f in range(fields):
            real = coef_ref[r, 2 * f : 2 * f + 1] * weights
            imag = coef_ref[r, 2 * f + 1 : 2 * f + 2] * weights
            for k in range(step_pad // 16):
                ec = e_ref[0, 16 * k : 16 * k + 16]
                es = e_ref[1, 16 * k : 16 * k + 16]
                at = f * step_pad + 16 * k
                for place, value in ((0, real * ec - imag * es), (slots, -(real * es + imag * ec))):
                    high, low = split(value)
                    w_ref[0, at : at + 16, place : place + slots] = high
                    w_ref[1, at : at + 16, place : place + slots] = low
        total = dot_nt(t_ref[0], w_ref[0]) + dot_nt(t_ref[0], w_ref[1]) + dot_nt(t_ref[1], w_ref[0])
        shape = total.shape
        point = lax.broadcasted_iota(jnp.int32, shape, 0) * step + lax.broadcasted_iota(jnp.int32, shape, 1) % step_pad
        total = jnp.where(point.astype(jnp.float32) < length, total, 0.0)[: lev_count * rows_dev]
        pieces = [total[:, f * step_pad : f * step_pad + step] for f in range(fields)]
        if wide > fields * step:
            pieces.append(jnp.zeros((lev_count * rows_dev, wide - fields * step), jnp.float32))
        send_ref[r] = jnp.concatenate(pieces, axis=1).reshape(lev_count, rows_dev, wide)
        if r == 0:
            pl.semaphore_wait(barrier, lev_count - 1)
        started = []
        for offset in range(1, lev_count):
            peer = lax.rem(me + offset, lev_count)
            copy = pltpu.make_async_remote_copy(
                src_ref=send_ref.at[r, peer],
                dst_ref=got_ref.at[r, me],
                send_sem=send_sem.at[r, offset],
                recv_sem=recv_sem.at[r, offset],
                device_id={"lev": peer},
                device_id_type=pl.DeviceIdType.MESH,
            )
            copy.start()
            started.append(copy)
        kept = pltpu.make_async_copy(send_ref.at[r, me], got_ref.at[r, me], own_sem.at[r])
        kept.start()
        started.append(kept)
        copies.append(started)

    group = lev_count * fields
    span = step * group
    source = lax.broadcasted_iota(jnp.int32, (wide, 1), 0)
    target = jnp.where(source < fields * step, (source % step) * group + source // step, -1)
    lane = lax.broadcasted_iota(jnp.int32, place_ref.shape, 1)
    place_ref[...] = jnp.where(lane == target, 1.0, 0.0).astype(jnp.bfloat16)
    for r in range(cycles):
        for copy in copies[r]:
            copy.wait()
        high, low = split(got_ref[r].reshape(lev_count * rows_dev, wide))
        spread = jnp.dot(high, place_ref[...], preferred_element_type=jnp.float32) + jnp.dot(
            low, place_ref[...], preferred_element_type=jnp.float32
        )
        total = spread[:rows_dev]
        for level in range(1, lev_count):
            total = total + pltpu.roll(spread[level * rows_dev : (level + 1) * rows_dev], fields * level, 1)
        for q in range(rows_dev):
            out_ref[r : r + 1, q * span : (q + 1) * span] = total[q : q + 1, :span]


def legendre_kernel(wave_ref, spec_ref, leg_ref, out_ref):
    parts, block, degrees = spec_ref.shape
    half_cycles = leg_ref.shape[0]
    table = leg_ref[...].reshape(half_cycles * block, degrees)
    waves = wave_ref[0]
    degree = lax.broadcasted_iota(jnp.int32, (block, degrees), 1)
    live = degree >= waves
    parity = (degree + waves) & 1
    values = spec_ref[...]
    cells = parts * block
    shape = (half_cycles, block, cells)
    own = lax.broadcasted_iota(jnp.int32, shape, 1) == lax.broadcasted_iota(jnp.int32, shape, 2) % block
    sums = []
    for which in (0, 1):
        mask = jnp.where(live & (parity == which), 1.0, 0.0).astype(jnp.bfloat16)
        part = (values * mask[None]).reshape(cells, degrees)
        product = dot_nt(table, part).reshape(shape)
        sums.append(jnp.sum(jnp.where(own, product, 0.0), axis=1))
    out_ref[0, 0] = sums[0] + sums[1]
    out_ref[0, 1] = sums[0] - sums[1]


def local(spectral, legendre, slot_wave, cycle_len, lat_order):
    slot_count = spectral.shape[2]
    degrees = spectral.shape[3]
    half_cycles = legendre.shape[1]
    wave_index = lax.axis_index("wave")
    lev_count = lax.axis_size("lev")
    wave_count = lax.axis_size("wave")
    slots = slot_wave.shape[0]
    padded_len = (RMAX + 8 * lev_count - 1) // (8 * lev_count) * 8 * lev_count
    points_dev = padded_len // lev_count
    step = points_dev // 8
    step_pad = (step + 15) // 16 * 16
    parts = spectral.shape[0] * spectral.shape[1]
    cycle_count = lat_order.shape[0] // wave_count

    local_waves = lax.dynamic_slice_in_dim(slot_wave, wave_index * slot_count, slot_count)
    block = 32 if slot_count % 32 == 0 else 16
    blocks = slot_count // block
    cells = parts * block
    fourier = pl.pallas_call(
        legendre_kernel,
        grid=(blocks,),
        out_shape=jax.ShapeDtypeStruct((blocks, 2, half_cycles, cells), jnp.float32),
        in_specs=[
            pl.BlockSpec((1, block, 1), lambda i: (i, 0, 0)),
            pl.BlockSpec((parts, block, degrees), lambda i: (0, i, 0)),
            pl.BlockSpec((half_cycles, block, degrees), lambda i: (0, i, 0)),
        ],
        out_specs=pl.BlockSpec((1, 2, half_cycles, cells), lambda i: (i, 0, 0, 0)),
        name="legendre",
    )(local_waves.reshape(blocks, block, 1), spectral.reshape(parts, slot_count, degrees), jnp.transpose(legendre, (1, 0, 2)))
    fourier = fourier.reshape(blocks, 2 * half_cycles, parts, block)
    fourier = jnp.transpose(fourier, (1, 2, 0, 3)).reshape(2 * half_cycles, parts * slot_count)
    ordered = jnp.take(fourier, lat_order, axis=0, mode="clip")
    ordered = ordered.reshape(wave_count, cycle_count, parts, slot_count)
    shared = lax.all_to_all(ordered, "wave", split_axis=0, concat_axis=0, tiled=True)
    coeffs = jnp.transpose(shared, (1, 2, 0, 3)).reshape(cycle_count, parts, slots)

    wide = (parts // 2 * step + 127) // 128 * 128
    span = (parts // 2 * lev_count * step + 127) // 128 * 128
    smem = pl.BlockSpec(memory_space=pltpu.SMEM)
    vmem = pl.BlockSpec(memory_space=pltpu.VMEM)
    row_pad = (lev_count + 1) // 2 * 16
    return pl.pallas_call(
        functools.partial(points_kernel, step, step_pad),
        out_shape=jax.ShapeDtypeStruct((cycle_count, points_dev * lev_count * (parts // 2)), jnp.float32),
        in_specs=[vmem, smem, smem, vmem],
        out_specs=vmem,
        scratch_shapes=[
            pltpu.VMEM((2, step_pad, slots), jnp.float32),
            pltpu.VMEM((2, parts // 2 * step_pad, 2 * slots), jnp.bfloat16),
            pltpu.VMEM((2, row_pad, 2 * slots), jnp.bfloat16),
            pltpu.VMEM((wide, span), jnp.bfloat16),
            pltpu.VMEM((cycle_count, lev_count, 8, wide), jnp.float32),
            pltpu.VMEM((cycle_count, lev_count, 8, wide), jnp.float32),
            pltpu.SemaphoreType.DMA((cycle_count,)),
            pltpu.SemaphoreType.DMA((cycle_count, lev_count)),
            pltpu.SemaphoreType.DMA((cycle_count, lev_count)),
        ],
        compiler_params=pltpu.CompilerParams(collective_id=0, has_side_effects=True),
        name="points",
    )(slot_wave[None, :], lat_order, cycle_len, coeffs)


def solution(mesh):
    in_specs = (P("lev", None, "wave", None), P("wave", None, None), P(), P(), P())
    out_specs = P("wave", "lev")
    return jax.shard_map(local, mesh=mesh, in_specs=in_specs, out_specs=out_specs, check_vma=False)
```

profile of v0, /device:TPU:0, one launch (start us, length us, event | category | flops | bytes accessed | tf_op | source)
XLA Modules:
  0.0 45.2 jit_solution(4006130793527475525)
XLA Ops:
  0.0 0.8 %dynamic_slice.3 = s32[320]{0:T(512)S(1)} dynamic-slice(s32[1280]{0:T(1024)} %param.7, s32[]{:T(128)S(6)} %select_n.3), dynamic_slice_sizes={320} | dynamic-slice | bytes 2564 | tf_op jit(solution)/shard_map/dynamic_slice | solution.py:184
  0.8 0.9 %reshape.33.wave_ref = s32[10,32,1]{2,1,0:T(8,128)} reshape(s32[320]{0:T(512)S(1)} %dynamic_slice.3) | data formatting | bytes 2560 | tf_op jit(solution)/shard_map/reshape | solution.py:199
  1.6 0.0 copy-start.1
  1.6 0.0 copy-start
  1.7 10.2 %legendre.1 = f32[10,2,6,192]{3,2,1,0:T(8,128)} custom-call(s32[10,32,1]{2,1,0:T(8,128)} %reshape.33.wave_ref, bf16[6,320,1280]{2,1,0:T(8,128)(2,1)} %bitcast.4, bf16[6,320,1280]{2,1,0:T(8,128)(2,1)} %bitcast.5), custom_call_target="tpu_custom_call" | custom-call | tf_op jit(solution)/shard_map/legendre/pallas_call | solution.py:188
  11.8 1.0 %reshape.20 = f32[10,12,6,32]{3,2,1,0:T(8,128)S(1)} reshape(f32[10,2,6,192]{3,2,1,0:T(8,128)} %legendre.1) | data formatting | bytes 184320 | tf_op jit(solution)/shard_map/reshape | solution.py:200
  12.9 0.2 copy.9
  13.1 0.2 reshape.21
  13.3 0.0 copy-done.1
  13.3 0.6 %gather_fusion = f32[12,1920]{1,0:T(8,128)S(1)} fusion(f32[12,1920]{1,0:T(8,128)S(1)} %reshape.21, s32[1024]{0:T(1024)S(1)} %pad_clamp_fusion), kind=kCustom, calls=%fused_computation | custom fusion | bytes 184368 | tf_op jit(solution)/shard_map/jit(_take)/gather | solution.py:202
  13.9 0.8 %reshape.22 = f32[4,3,6,320]{3,2,1,0:T(8,128)} reshape(f32[12,1920]{1,0:T(8,128)S(1)} %gather_fusion) | data formatting | bytes 184320 | tf_op jit(solution)/shard_map/reshape | solution.py:203
  14.7 4.3 %all-to-all-start = ((f32[4,3,6,320]{3,2,1,0:T(8,128)}), f32[4,3,6,320]{3,2,1,0:T(8,128)S(1)}, u32[]{:S(2)}, u32[]{:S(2)}) async-start(f32[4,3,6,320]{3,2,1,0:T(8,128)} %reshape.22), calls=%async_computation | async-start | bytes 294912 | tf_op jit(solution)/shard_map/all_to_all | solution.py:204
  18.9 0.0 copy-done
  18.9 0.6 %broadcast_in_dim.7.wave_ref = s32[1,1280]{1,0:T(1,128)} reshape(s32[1280]{0:T(1024)S(1)} %copy-done) | data formatting | bytes 10240 | tf_op jit(solution)/shard_map/broadcast_in_dim | solution.py:230
  19.5 4.2 %all-to-all-done = f32[4,3,6,320]{3,2,1,0:T(8,128)S(1)} async-done(((f32[4,3,6,320]{3,2,1,0:T(8,128)}), f32[4,3,6,320]{3,2,1,0:T(8,128)S(1)}, u32[]{:S(2)}, u32[]{:S(2)}) %all-to-all-start) | async-done | bytes 92192 | tf_op jit(solution)/shard_map/all_to_all | solution.py:204
  23.7 0.8 %reshape.23.coef_ref = f32[3,6,1280]{2,1,0:T(8,128)} reshape(f32[3,6,4,320]{3,2,1,0:T(4,128)S(1)} %copy.10) | data formatting | bytes 184320 | tf_op jit(solution)/shard_map/reshape | solution.py:205
  24.5 19.0 %points.1 = f32[3,15552]{1,0:T(4,128)} custom-call(s32[1,1280]{1,0:T(1,128)} %broadcast_in_dim.7.wave_ref, s32[12]{0:T(128)} %lat_ref.1, s32[6]{0:T(128)} %cycle_ref.1, f32[3,6,1280]{2,1,0:T(8,128)} %reshape.23.coef_ref), custom_call_target="tpu_custom_call" | custom-call | tf_op jit(solution)/shard_map/points/pallas_call | solution.py:212
  43.5 1.7 %copy.12 = f32[3,15552]{1,0:T(4,128)} copy(f32[3,15552]{1,0:T(4,128)} %points.1) | data formatting | bytes 373248
  (2 shorter events, 0.0 us)
Async XLA Ops:
  1.6 11.6 %copy-start.1 = (s32[12]{0:T(128)S(1)}, s32[12]{0:T(128)}, u32[]{:S(2)}) copy-start(s32[12]{0:T(128)} %lat_ref.1) | copy-start | bytes 148
  1.6 17.3 %copy-start = (s32[1280]{0:T(1024)S(1)}, s32[1280]{0:T(1024)}, u32[]{:S(2)}) copy-start(s32[1280]{0:T(1024)} %param.7) | copy-start | bytes 15364
  14.7 9.0 %all-to-all-start = ((f32[4,3,6,320]{3,2,1,0:T(8,128)}), f32[4,3,6,320]{3,2,1,0:T(8,128)S(1)}, u32[]{:S(2)}, u32[]{:S(2)}) async-start(f32[4,3,6,320]{3,2,1,0:T(8,128)} %reshape.22), calls=%async_computation | async-start | bytes 294912 | tf_op jit(solution)/shard_map/all_to_all | solution.py:204
where the time goes:
time: 45.8 us; the launch traced here: 45.2 us
  Pallas kernels  29.2 us (64%)
  local copies, waits for them, and re-layouts  7.53 us (16%)
  starting transfers between devices  4.27 us (9%)
  waiting for transfers between devices  4.18 us (9%)
    pallas_call x1, Pallas kernels, local(): pl.pallas_call(functools.partial(points_kernel, step, step_pad), out_shap...  19 us
    pallas_call x1, Pallas kernels, local(): pl.pallas_call(legendre_kernel, grid=(blocks,), out_shape=jax.ShapeDtypeS...  10.2 us
    all_to_all x1, starting transfers between devices, local(): lax.all_to_all(ordered, 'wave', split_axis=0, concat_axis=0, tiled=True)  4.27 us
    all_to_all x1, waiting for transfers between devices, local(): lax.all_to_all(ordered, 'wave', split_axis=0, concat_axis=0, tiled=True)  4.18 us
    unnamed x5, local copies, waits for them, and re-layouts  1.69 us
    reshape x1, local copies, waits for them, and re-layouts, local(): fourier = fourier.reshape(blocks, 2 * half_cycles, parts, block)  1.04 us
  transfers between devices with their start and end apart: 1, of which 1 were waited for; matrix products, arithmetic and copies ran while one was open for 1% of the time, Pallas kernels for 0%

commit v1 on v0

v1 whole, which is shorter than its diff:
```python
import functools
import math

import jax
import jax.numpy as jnp
from jax import lax
from jax.experimental import pallas as pl
from jax.experimental.pallas import tpu as pltpu
from jax.sharding import PartitionSpec as P

RMAX = 5136
LANES = 128
BLOCK = 16


def split(value):
    high = value.astype(jnp.bfloat16)
    return high, (value - high.astype(jnp.float32)).astype(jnp.bfloat16)


def dot_nt(left, right):
    return lax.dot_general(left, right, (((1,), (1,)), ((), ())), preferred_element_type=jnp.float32)


def turns(t):
    y = math.pi * t
    z = y * y
    sine = jnp.full_like(z, 1.0 / math.factorial(13))
    for n in (11, 9, 7, 5, 3, 1):
        sign = -1.0 if (n // 2) % 2 else 1.0
        sine = sine * z + sign / math.factorial(n)
    sine = sine * y
    cosine = jnp.full_like(z, 1.0 / math.factorial(12))
    for n in (10, 8, 6, 4, 2, 0):
        sign = -1.0 if (n // 2) % 2 else 1.0
        cosine = cosine * z + sign / math.factorial(n)
    return 1.0 - 2.0 * sine * sine, 2.0 * sine * cosine


def iota(shape, dim):
    return lax.broadcasted_iota(jnp.int32, shape, dim)


def kernel(
    half_step, chunk,
    wave_ref, lat_ref, cycle_ref, spec_hbm, leg_hbm, out_ref,
    spec_ref, leg_ref, col_ref, four_ref, wsend_ref, wgot_ref,
    twist_ref, cen_ref, tab_ref, u_ref, place_ref, send_ref, got_ref,
    load_sem, wown_sem, wsend_sem, wrecv_sem, own_sem, send_sem, recv_sem,
):
    parts, slot_count, degrees = spec_ref.shape
    half_cycles = leg_ref.shape[0]
    fields = parts // 2
    groups, wave_count, cycles = wsend_ref.shape[:3]
    lev_count = send_ref.shape[1]
    wide = send_ref.shape[-1]
    slots = wave_ref.shape[0]
    tiles = slots // LANES
    step = 2 * half_step
    points_dev = 4 * step
    half_rows = twist_ref.shape[2]
    blocks = half_rows // 8
    counts = (half_step + 15) // 16
    low_at = tab_ref.shape[2] - 16 * counts
    me = lax.axis_index("lev")
    my_wave = lax.axis_index("wave")
    first_row = my_wave * cycles

    barrier = pltpu.get_barrier_semaphore()
    for offset in range(1, lev_count):
        peer = lax.rem(me + offset, lev_count)
        pl.semaphore_signal(barrier, inc=1, device_id={"lev": peer}, device_id_type=pl.DeviceIdType.MESH)
    for offset in range(1, wave_count):
        peer = lax.rem(my_wave + offset, wave_count)
        pl.semaphore_signal(barrier, inc=1, device_id={"wave": peer}, device_id_type=pl.DeviceIdType.MESH)

    loads = []
    for i in range(slot_count // chunk):
        at = pl.ds(i * chunk, chunk)
        pair = [
            pltpu.make_async_copy(leg_hbm.at[:, at], leg_ref.at[:, at], load_sem.at[0, i]),
            pltpu.make_async_copy(spec_hbm.at[:, at], spec_ref.at[:, at], load_sem.at[1, i]),
        ]
        for copy in pair:
            copy.start()
        loads.append(pair)

    waves = wave_ref[...].reshape(1, slots).astype(jnp.float32)

    mine = pltpu.roll(waves, slots - my_wave * slot_count, 1)
    eye = iota((LANES, LANES), 0) == iota((LANES, LANES), 1)
    for g in range(groups):
        column = jnp.sum(jnp.where(eye, mine[:, g * LANES : (g + 1) * LANES], 0.0), axis=1, keepdims=True)
        col_ref[g * LANES : (g + 1) * LANES] = jnp.broadcast_to(column, (LANES, LANES))

    near = [i + 0.5 for i in range(8)]
    twist = [step * (i + 0.5) for i in range(8)]
    rest = [16.0 * k + 8.0 for k in range(counts)] + [8.0 * step * a for a in range(1, blocks)]
    rest += [(lev_count * points_dev - 1) / 2]
    rest_count = len(rest)
    rest_rows = (rest_count + 7) // 8 * 8
    row = iota((rest_rows, 1), 0)
    row8 = iota((8, 1), 0).astype(jnp.float32) + 0.5
    rest_mult = jnp.zeros((rest_rows, 1), jnp.float32)
    for i, value in enumerate(rest):
        rest_mult = jnp.where(row == i, value, rest_mult)
    mult = jnp.concatenate([row8, row8 * step, rest_mult], axis=0)
    lengths = [
        cycle_ref[lat_ref[first_row + r] % half_cycles].astype(jnp.float32) for r in range(cycles)
    ]
    if low_at > 16 * counts:
        hole = low_at - 16 * counts
        tab_ref[:, :, 16 * counts : low_at] = jnp.zeros((cycles, 2, hole, slots), jnp.bfloat16)

    def tables(r, t):
        at = slice(t * LANES, (t + 1) * LANES)
        wave = waves[:, at]
        length = lengths[r]
        inverse = 1.0 / jnp.full((1, LANES), length)
        phase = wave * mult
        whole = jnp.floor(phase * inverse + 0.5)
        cosine, sine = turns((phase - whole * length) * inverse)
        nc, ns, tc, ts = cosine[0:8], sine[0:8], cosine[8:16], sine[8:16]
        rc, rs = cosine[16:], sine[16:]
        twist_ref[r, 0, 0:8, at] = tc
        twist_ref[r, 1, 0:8, at] = ts
        for a in range(1, blocks):
            i = counts + a - 1
            c, s = rc[i : i + 1], rs[i : i + 1]
            twist_ref[r, 0, 8 * a : 8 * a + 8, at] = tc * c - ts * s
            twist_ref[r, 1, 8 * a : 8 * a + 8, at] = ts * c + tc * s
        weight = jnp.where(wave == 0.0, 1.0, 2.0)
        i = rest_count - 1
        cen_ref[r, 0:1, at] = rc[i : i + 1] * weight
        cen_ref[r, 1:2, at] = rs[i : i + 1] * weight
        for k in range(counts):
            c, s = rc[k : k + 1], rs[k : k + 1]
            cc, ss, sc, cs = c * nc, s * ns, s * nc, c * ns
            for which, value in (
                (0, jnp.concatenate([cc + ss, cc - ss], axis=0)),
                (1, jnp.concatenate([sc - cs, sc + cs], axis=0)),
            ):
                high, low = split(value)
                tab_ref[r, which, 16 * k : 16 * k + 16, at] = high
                tab_ref[r, which, low_at + 16 * k : low_at + 16 * k + 16, at] = low

    chunks = LANES // BLOCK
    lane = iota((1, LANES), 1)
    lane_chunk = lane // BLOCK
    degree = iota((BLOCK, degrees), 1)
    flip = jnp.where((iota((BLOCK, degrees), 1) & 1) == 1, -1.0, 1.0).astype(jnp.bfloat16)
    own = iota((BLOCK, LANES), 0) == iota((BLOCK, LANES), 1) % BLOCK
    lats = 2 * half_cycles

    def legendre(b, turn):
        at = slice(b * BLOCK, (b + 1) * BLOCK)
        column = col_ref[at, 0:1].astype(jnp.int32)
        live = jnp.where(degree >= column, 1.0, 0.0).astype(jnp.bfloat16)
        north = leg_ref[:, at, :] * live[None]
        south = north * flip[None]
        table = jnp.concatenate([north, south], axis=0).reshape(lats * BLOCK, degrees)
        order = [(j - turn) % chunks for j in range(chunks)]
        rows = jnp.concatenate([spec_ref[c if c < parts else 0, at, :] for c in order], axis=0)
        product = dot_nt(table, rows).reshape(lats, BLOCK, LANES)
        return jnp.sum(jnp.where(own[None], product, 0.0), axis=1)

    wave_copies = []

    def send_group(g, sums):
        sign = jnp.where(
            (iota((lats, 1), 0) >= half_cycles)
            & ((mine[:, g * LANES : (g + 1) * LANES].astype(jnp.int32) & 1) == 1),
            -1.0,
            1.0,
        )
        for c in range(parts):
            picked = sums[0]
            for b in range(1, len(sums)):
                picked = jnp.where(lane_chunk == (c + b) % chunks, sums[b], picked)
            if c:
                picked = pltpu.roll(picked, LANES - c * BLOCK, 1)
            four_ref[:, (c % 2) * 4 + c // 2, :] = picked * sign
        for w in range(wave_count):
            for r in range(cycles):
                wsend_ref[g, w, r] = four_ref[lat_ref[w * cycles + r]]
        if g == 0:
            pl.semaphore_wait(barrier, lev_count + wave_count - 2)
        for offset in range(1, wave_count):
            peer = lax.rem(my_wave + offset, wave_count)
            copy = pltpu.make_async_remote_copy(
                src_ref=wsend_ref.at[g, peer],
                dst_ref=wgot_ref.at[g, my_wave],
                send_sem=wsend_sem.at[g, offset],
                recv_sem=wrecv_sem.at[g, offset],
                device_id={"wave": peer},
                device_id_type=pl.DeviceIdType.MESH,
            )
            copy.start()
            wave_copies.append(copy)
        kept = pltpu.make_async_copy(wsend_ref.at[g, my_wave], wgot_ref.at[g, my_wave], wown_sem.at[g])
        kept.start()
        wave_copies.append(kept)

    todo = [(r, t) for r in range(cycles) for t in range(tiles)]
    ahead = todo[: 2 * tiles]
    total_blocks = slot_count // BLOCK
    done = 0
    sums = []
    for b in range(total_blocks):
        if b * BLOCK % chunk == 0:
            for copy in loads[b * BLOCK // chunk]:
                copy.wait()
        sums.append(legendre(b, b % chunks))
        if b % chunks == chunks - 1 or b == total_blocks - 1:
            send_group(b // chunks, sums)
            sums = []
        upto = len(ahead) * (b + 1) // total_blocks
        for r, t in ahead[done:upto]:
            tables(r, t)
        done = upto
    for r, t in todo[2 * tiles :]:
        tables(r, t)

    group = lev_count * fields
    span = half_step * group
    source = iota((wide, 1), 0)
    target = jnp.where(source < fields * half_step, (source % half_step) * group + source // half_step, -1)
    for j in range(place_ref.shape[1] // LANES):
        at = slice(j * LANES, (j + 1) * LANES)
        place_ref[:, at] = jnp.where(iota((wide, LANES), 1) + j * LANES == target, 1.0, 0.0).astype(jnp.bfloat16)

    picks = {}
    for f in range(fields):
        point = (lane + (LANES - f * half_step % LANES)) % LANES
        for back in (0, 1):
            p = half_step - 1 - point if back else point
            p = jnp.clip(p, 0, half_step - 1)
            low = p % 16
            index = p - low + jnp.where(low < 8, 7 - low, low)
            picks[f, back] = jnp.broadcast_to(index, (half_rows, LANES))
    where_lane = iota((8, wide), 1)
    where_row = iota((8, wide), 0)
    inside = jnp.where(where_lane < fields * half_step, where_lane % half_step, 1 << 20)
    reach = {}
    for upper in (0, 1):
        i = where_row % 4 if upper else 3 - where_row % 4
        reach[upper] = (step * i + half_step * (where_row // 4) + inside).astype(jnp.float32)

    for copy in wave_copies:
        copy.wait()

    copies = []
    turn_sign = jnp.where(iota((8, 1), 0) < 4, -1.0, 1.0)
    for r in range(cycles):
        for t in range(tiles):
            at = slice(t * LANES, (t + 1) * LANES)
            coef = None
            position = t * LANES
            while position < (t + 1) * LANES:
                w, inner = position // slot_count, position % slot_count
                g, start = inner // LANES, inner % LANES
                size = min((t + 1) * LANES - position, slot_count - inner, LANES - start)
                piece = wgot_ref[g, w, r]
                to = position - t * LANES
                if to != start:
                    piece = pltpu.roll(piece, (to - start) % LANES, 1)
                coef = piece if coef is None else jnp.where(lane >= to, piece, coef)
                position += size
            coef = coef * cen_ref[r, 0:1, at] + pltpu.roll(coef, 4, 0) * (cen_ref[r, 1:2, at] * turn_sign)
            tc, ts = twist_ref[r, 0, :, at], twist_ref[r, 1, :, at]
            for f in range(fields):
                real, imag = coef[f : f + 1], coef[4 + f : 5 + f]
                for which, first, value in ((0, 0, real * tc), (0, 1, imag * ts), (1, 0, real * ts), (1, 1, imag * tc)):
                    high, low = split(value)
                    base = (first * fields + f) * half_rows
                    u_ref[which, base : base + half_rows, at] = high
                    base += 2 * fields * half_rows
                    u_ref[which, base : base + half_rows, at] = low
        both = []
        rows = 2 * fields * half_rows
        for which in (0, 1):
            product = dot_nt(u_ref[which], tab_ref[r, which])
            value = product[:rows] + product[rows:]
            both.append(value[:, :LANES] + jnp.concatenate([value[:, low_at:], jnp.zeros((rows, low_at - 16 * counts), jnp.float32)], axis=1))
        mixed = {}
        for f in range(fields):
            p1, p2 = (both[0][(i * fields + f) * half_rows : (i * fields + f + 1) * half_rows] for i in (0, 1))
            p3, p4 = (both[1][(i * fields + f) * half_rows : (i * fields + f + 1) * half_rows] for i in (0, 1))
            even_up, odd_up = p1 - p2, p3 + p4
            even_down, odd_down = p1 + p2, p4 - p3
            for upper, even, odd in ((1, even_up, odd_up), (0, even_down, odd_down)):
                for back, value in ((0, even - odd), (1, even + odd)):
                    mixed[upper, back, f] = jnp.take_along_axis(
                        value, picks[f, back], axis=1, mode="promise_in_bounds"
                    )
        for upper in (0, 1):
            row_tiles = []
            for back in (1, 0):
                pieces = []
                for j in range(wide // LANES):
                    piece = None
                    for f in range(fields):
                        start, stop = f * half_step - j * LANES, (f + 1) * half_step - j * LANES
                        if stop <= 0 or start >= LANES:
                            continue
                        value = mixed[upper, back, f]
                        piece = value if piece is None else jnp.where(lane >= start, value, piece)
                    pieces.append(piece)
                row_tiles.append(jnp.concatenate(pieces, axis=1))
            for a in range(lev_count // 2):
                dest = lev_count // 2 + a if upper else lev_count // 2 - 1 - a
                tile = jnp.concatenate([value[4 * a : 4 * a + 4] for value in row_tiles], axis=0)
                send_ref[r, dest] = jnp.where(reach[upper] < lengths[r] - float(points_dev * dest), tile, 0.0)
        started = []
        offsets = sorted(range(1, lev_count), key=lambda o: abs(o - lev_count / 2))
        for offset in offsets:
            peer = lax.rem(me + offset, lev_count)
            copy = pltpu.make_async_remote_copy(
                src_ref=send_ref.at[r, peer],
                dst_ref=got_ref.at[r, me],
                send_sem=send_sem.at[r, offset],
                recv_sem=recv_sem.at[r, offset],
                device_id={"lev": peer},
                device_id_type=pl.DeviceIdType.MESH,
            )
            copy.start()
            started.append(copy)
        kept = pltpu.make_async_copy(send_ref.at[r, me], got_ref.at[r, me], own_sem.at[r])
        kept.start()
        started.append(kept)
        copies.append(started)

    upper = me >= lev_count // 2
    sub = iota((8, place_ref.shape[1]), 0)
    order = jnp.where(upper, sub, (sub // 4) * 4 + 3 - sub % 4)
    for r in range(cycles):
        for copy in copies[r]:
            copy.wait()
        high, low = split(got_ref[r].reshape(lev_count * 8, wide))
        spread = jnp.dot(high, place_ref[...], preferred_element_type=jnp.float32) + jnp.dot(
            low, place_ref[...], preferred_element_type=jnp.float32
        )
        total = spread[:8]
        for level in range(1, lev_count):
            total = total + pltpu.roll(spread[level * 8 : (level + 1) * 8], fields * level, 1)
        total = jnp.take_along_axis(total, order, axis=0, mode="promise_in_bounds")
        for q in range(8):
            s = (q % 2) * 4 + q // 2
            out_ref[r : r + 1, q * span : (q + 1) * span] = total[s : s + 1, :span]


def local(spectral, legendre, slot_wave, cycle_len, lat_order):
    slot_count = spectral.shape[2]
    degrees = spectral.shape[3]
    half_cycles = legendre.shape[1]
    lev_count = lax.axis_size("lev")
    wave_count = lax.axis_size("wave")
    slots = slot_wave.shape[0]
    padded_len = (RMAX + 8 * lev_count - 1) // (8 * lev_count) * 8 * lev_count
    points_dev = padded_len // lev_count
    half_step = points_dev // 8
    parts = spectral.shape[0] * spectral.shape[1]
    fields = parts // 2
    cycles = lat_order.shape[0] // wave_count
    groups = (slot_count + LANES - 1) // LANES
    chunk = 32 if slot_count % 32 == 0 else 16
    half_rows = 2 * lev_count
    counts = (half_step + 15) // 16
    low_at = (16 * counts + LANES - 1) // LANES * LANES

    wide = (fields * half_step + LANES - 1) // LANES * LANES
    span = (fields * lev_count * half_step + LANES - 1) // LANES * LANES
    smem = pl.BlockSpec(memory_space=pltpu.SMEM)
    vmem = pl.BlockSpec(memory_space=pltpu.VMEM)
    hbm = pl.BlockSpec(memory_space=pl.ANY)
    return pl.pallas_call(
        functools.partial(kernel, half_step, chunk),
        out_shape=pltpu.VMEM((cycles, points_dev * lev_count * fields), jnp.float32),
        in_specs=[vmem, smem, smem, hbm, hbm],
        out_specs=vmem,
        scratch_shapes=[
            pltpu.VMEM((parts, slot_count, degrees), jnp.bfloat16),
            pltpu.VMEM((half_cycles, slot_count, degrees), jnp.bfloat16),
            pltpu.VMEM((groups * LANES, LANES), jnp.float32),
            pltpu.VMEM((2 * half_cycles, 8, LANES), jnp.float32),
            pltpu.VMEM((groups, wave_count, cycles, 8, LANES), jnp.float32),
            pltpu.VMEM((groups, wave_count, cycles, 8, LANES), jnp.float32),
            pltpu.VMEM((cycles, 2, half_rows, slots), jnp.float32),
            pltpu.VMEM((cycles, 8, slots), jnp.float32),
            pltpu.VMEM((cycles, 2, low_at + 16 * counts, slots), jnp.bfloat16),
            pltpu.VMEM((2, 4 * fields * half_rows, slots), jnp.bfloat16),
            pltpu.VMEM((wide, span), jnp.bfloat16),
            pltpu.VMEM((cycles, lev_count, 8, wide), jnp.float32),
            pltpu.VMEM((cycles, lev_count, 8, wide), jnp.float32),
            pltpu.SemaphoreType.DMA((2, slot_count // chunk)),
            pltpu.SemaphoreType.DMA((groups,)),
            pltpu.SemaphoreType.DMA((groups, wave_count)),
            pltpu.SemaphoreType.DMA((groups, wave_count)),
            pltpu.SemaphoreType.DMA((cycles,)),
            pltpu.SemaphoreType.DMA((cycles, lev_count)),
            pltpu.SemaphoreType.DMA((cycles, lev_count)),
        ],
        compiler_params=pltpu.CompilerParams(collective_id=0, has_side_effects=True),
        name="transform",
    )(
        slot_wave, lat_order, cycle_len,
        spectral.reshape(parts, slot_count, degrees), jnp.transpose(legendre, (1, 0, 2)),
    )


def solution(mesh):
    in_specs = (P("lev", None, "wave", None), P("wave", None, None), P(), P(), P())
    out_specs = P("wave", "lev")
    return jax.shard_map(local, mesh=mesh, in_specs=in_specs, out_specs=out_specs, check_vma=False)
```

time: 45.8 us -> 24 us (0.52)
  local copies, waits for them, and re-layouts: 7.53 us -> 0.7 us
  Pallas kernels: 29.2 us -> 23.1 us
  starting transfers between devices: 4.27 us -> 0 us
  waiting for transfers between devices: 4.18 us -> 0 us
    pallas_call x2 -> x1, Pallas kernels: 29.2 us -> 23.1 us  [local(): pl.pallas_call(functools.partial(kernel, half_step, chunk), out_shape=plt...]
    all_to_all x1 -> x0, starting transfers between devices: 4.27 us -> none  [local(): lax.all_to_all(ordered, 'wave', split_axis=0, concat_axis=0, tiled=True)]
    all_to_all x1 -> x0, waiting for transfers between devices: 4.18 us -> none  [local(): lax.all_to_all(ordered, 'wave', split_axis=0, concat_axis=0, tiled=True)]
    reshape x5 -> x0, local copies, waits for them, and re-layouts: 3.62 us -> none  [the longest x1 1.04 us: local(): fourier = fourier.reshape(blocks, 2 * half_cycles, parts, block)]
    unnamed x5 -> x1, local copies, waits for them, and re-layouts: 1.69 us -> 0.7 us
    dynamic_slice x1 -> x0, local copies, waits for them, and re-layouts: 0.77 us -> none  [local(): lax.dynamic_slice_in_dim(slot_wave, wave_index * slot_count, slot_count)]
    broadcast_in_dim x1 -> x0, local copies, waits for them, and re-layouts: 0.6 us -> none  [local(): slot_wave[None, :]]
    gather x1 -> x0, local copies, waits for them, and re-layouts: 0.59 us -> none  [local(): ordered = jnp.take(fourier, lat_order, axis=0, mode='clip')]
  transfers between devices with their start and end apart: 1 -> 0, of which waited for: 1 -> 0; matrix products, arithmetic and copies ran while one was open for 1% -> 0% of each run, Pallas kernels for 0% -> 0%
where the time goes in v1:
time: 24 us; the launch traced here: 23.8 us
  Pallas kernels  23.1 us (96%)
  local copies, waits for them, and re-layouts  0.7 us (3%)
    pallas_call x1, Pallas kernels, local(): pl.pallas_call(functools.partial(kernel, half_step, chunk), out_shape=plt...  23.1 us
    unnamed x1, local copies, waits for them, and re-layouts  0.7 us

profile of v1, /device:TPU:0, one launch (start us, length us, event | category | flops | bytes accessed | tf_op | source)
XLA Modules:
  0.0 23.8 jit_solution(8497608865076455649)
XLA Ops:
  0.0 23.1 %transform.1 = f32[3,15552]{1,0:T(4,128)S(1)} custom-call(s32[1280]{0:T(1024)} %wave_ref.1, s32[12]{0:T(128)} %lat_ref.1, s32[6]{0:T(128)} %cycle_ref.1, bf16[6,320,1280]{2,1,0:T(8,128)(2,1)} %bitcast.2, bf16[6,320,1280]{2,1,0:T(8,128)(2,1)} %bitcast.3), custom_call_target="tpu_custom_call" | custom-call | tf_op jit(solution)/shard_map/transform/pallas_call | solution.py:376
  23.1 0.7 %copy.7 = f32[3,15552]{1,0:T(4,128)} copy(f32[3,15552]{1,0:T(4,128)S(1)} %transform.1) | data formatting | bytes 373248

commit v2 on v1

--- a/solution.py
+++ b/solution.py
@@ -45,7 +45,7 @@
     half_step, chunk,
     wave_ref, lat_ref, cycle_ref, spec_hbm, leg_hbm, out_ref,
     spec_ref, leg_ref, col_ref, four_ref, wsend_ref, wgot_ref,
-    twist_ref, cen_ref, tab_ref, u_ref, place_ref, send_ref, got_ref,
+    twist_ref, cen_ref, tab_ref, place_ref, send_ref, got_ref,
     load_sem, wown_sem, wsend_sem, wrecv_sem, own_sem, send_sem, recv_sem,
 ):
     parts, slot_count, degrees = spec_ref.shape
@@ -61,7 +61,7 @@
     half_rows = twist_ref.shape[2]
     blocks = half_rows // 8
     counts = (half_step + 15) // 16
-    low_at = tab_ref.shape[2] - 16 * counts
+    low_at = tab_ref.shape[3] - 16 * counts
     me = lax.axis_index("lev")
     my_wave = lax.axis_index("wave")
     first_row = my_wave * cycles
@@ -91,7 +91,7 @@
     eye = iota((LANES, LANES), 0) == iota((LANES, LANES), 1)
     for g in range(groups):
         column = jnp.sum(jnp.where(eye, mine[:, g * LANES : (g + 1) * LANES], 0.0), axis=1, keepdims=True)
-        col_ref[g * LANES : (g + 1) * LANES] = jnp.broadcast_to(column, (LANES, LANES))
+        col_ref[g * LANES : (g + 1) * LANES] = column - iota((LANES, LANES), 1).astype(jnp.float32)
 
     near = [i + 0.5 for i in range(8)]
     twist = [step * (i + 0.5) for i in range(8)]
@@ -110,7 +110,7 @@
     ]
     if low_at > 16 * counts:
         hole = low_at - 16 * counts
-        tab_ref[:, :, 16 * counts : low_at] = jnp.zeros((cycles, 2, hole, slots), jnp.bfloat16)
+        tab_ref[:, :, :, 16 * counts : low_at, :] = jnp.zeros((cycles, 2, tiles, hole, LANES), jnp.bfloat16)
 
     def tables(r, t):
         at = slice(t * LANES, (t + 1) * LANES)
@@ -141,45 +141,59 @@
                 (1, jnp.concatenate([sc - cs, sc + cs], axis=0)),
             ):
                 high, low = split(value)
-                tab_ref[r, which, 16 * k : 16 * k + 16, at] = high
-                tab_ref[r, which, low_at + 16 * k : low_at + 16 * k + 16, at] = low
+                tab_ref[r, which, t, 16 * k : 16 * k + 16, :] = high
+                tab_ref[r, which, t, low_at + 16 * k : low_at + 16 * k + 16, :] = low
 
     chunks = LANES // BLOCK
     lane = iota((1, LANES), 1)
     lane_chunk = lane // BLOCK
-    degree = iota((BLOCK, degrees), 1)
     flip = jnp.where((iota((BLOCK, degrees), 1) & 1) == 1, -1.0, 1.0).astype(jnp.bfloat16)
-    own = iota((BLOCK, LANES), 0) == iota((BLOCK, LANES), 1) % BLOCK
     lats = 2 * half_cycles
+    own = iota((BLOCK, lats * BLOCK), 0) == iota((BLOCK, lats * BLOCK), 1) % BLOCK
 
     def legendre(b, turn):
         at = slice(b * BLOCK, (b + 1) * BLOCK)
-        column = col_ref[at, 0:1].astype(jnp.int32)
-        live = jnp.where(degree >= column, 1.0, 0.0).astype(jnp.bfloat16)
+        column = col_ref[at, :]
+        live = jnp.concatenate(
+            [jnp.where(column <= float(d), 1.0, 0.0) for d in range(0, degrees, LANES)], axis=1
+        ).astype(jnp.bfloat16)
         north = leg_ref[:, at, :] * live[None]
         south = north * flip[None]
-        table = jnp.concatenate([north, south], axis=0).reshape(lats * BLOCK, degrees)
-        order = [(j - turn) % chunks for j in range(chunks)]
-        rows = jnp.concatenate([spec_ref[c if c < parts else 0, at, :] for c in order], axis=0)
-        product = dot_nt(table, rows).reshape(lats, BLOCK, LANES)
-        return jnp.sum(jnp.where(own[None], product, 0.0), axis=1)
+        both = (north, south)
+        order = [(j - turn) % lats for j in range(lats)]
+        table = jnp.concatenate([both[j // half_cycles][j % half_cycles] for j in order], axis=0)
+        product = dot_nt(spec_ref[:, at, :].reshape(parts * BLOCK, degrees), table)
+        product = product.reshape(parts, BLOCK, lats * BLOCK)
+        total = jnp.sum(jnp.where(own[None], product, 0.0), axis=1)
+        extra = -total.shape[1] % LANES
+        if extra:
+            total = jnp.concatenate([total, jnp.zeros((parts, extra), jnp.float32)], axis=1)
+        return [total[:, j * LANES : (j + 1) * LANES] for j in range(total.shape[1] // LANES)]
 
     wave_copies = []
 
     def send_group(g, sums):
-        sign = jnp.where(
-            (iota((lats, 1), 0) >= half_cycles)
-            & ((mine[:, g * LANES : (g + 1) * LANES].astype(jnp.int32) & 1) == 1),
-            -1.0,
-            1.0,
-        )
-        for c in range(parts):
-            picked = sums[0]
-            for b in range(1, len(sums)):
-                picked = jnp.where(lane_chunk == (c + b) % chunks, sums[b], picked)
-            if c:
-                picked = pltpu.roll(picked, LANES - c * BLOCK, 1)
-            four_ref[:, (c % 2) * 4 + c // 2, :] = picked * sign
+        sign = jnp.where((mine[:, g * LANES : (g + 1) * LANES].astype(jnp.int32) & 1) == 1, -1.0, 1.0)
+        for j in range(lats):
+            shifts = {}
+            for b, total in enumerate(sums):
+                place = (j + b) % lats
+                shifts.setdefault((b - place) % chunks, []).append((b, place % chunks, total[place // chunks]))
+            value = None
+            for shift, members in shifts.items():
+                picked = None
+                for b, at_chunk, total in members:
+                    picked = total if picked is None else jnp.where(lane_chunk == at_chunk, total, picked)
+                if shift:
+                    picked = pltpu.roll(picked, shift * BLOCK, 1)
+                first, last = members[0][0], members[-1][0]
+                if value is None:
+                    value = picked
+                else:
+                    value = jnp.where((lane_chunk >= first) & (lane_chunk <= last), picked, value)
+            if j >= half_cycles:
+                value = value * sign
+            four_ref[j, 0:parts, :] = value
         for w in range(wave_count):
             for r in range(cycles):
                 wsend_ref[g, w, r] = four_ref[lat_ref[w * cycles + r]]
@@ -201,8 +215,9 @@
         kept.start()
         wave_copies.append(kept)
 
-    todo = [(r, t) for r in range(cycles) for t in range(tiles)]
-    ahead = todo[: 2 * tiles]
+    for t in range(tiles):
+        tables(0, t)
+    ahead = [(r, t) for r in range(1, min(2, cycles)) for t in range(tiles)]
     total_blocks = slot_count // BLOCK
     done = 0
     sums = []
@@ -211,47 +226,59 @@
             for copy in loads[b * BLOCK // chunk]:
                 copy.wait()
         sums.append(legendre(b, b % chunks))
-        if b % chunks == chunks - 1 or b == total_blocks - 1:
-            send_group(b // chunks, sums)
-            sums = []
         upto = len(ahead) * (b + 1) // total_blocks
         for r, t in ahead[done:upto]:
             tables(r, t)
         done = upto
-    for r, t in todo[2 * tiles :]:
-        tables(r, t)
+        if b % chunks == chunks - 1 or b == total_blocks - 1:
+            send_group(b // chunks, sums)
+            sums = []
+    for r in range(2, cycles):
+        for t in range(tiles):
+            tables(r, t)
 
     group = lev_count * fields
-    span = half_step * group
-    source = iota((wide, 1), 0)
-    target = jnp.where(source < fields * half_step, (source % half_step) * group + source // half_step, -1)
+    quarter = (half_step + 3) // 4
+    source = iota((4 * 64, 1), 0)
+    inner = source % 64
+    target = jnp.where(
+        inner < fields * quarter, (inner % quarter) * group + source // 64 * fields + inner // quarter, -1
+    )
     for j in range(place_ref.shape[1] // LANES):
         at = slice(j * LANES, (j + 1) * LANES)
-        place_ref[:, at] = jnp.where(iota((wide, LANES), 1) + j * LANES == target, 1.0, 0.0).astype(jnp.bfloat16)
+        place_ref[:, at] = jnp.where(iota((4 * 64, LANES), 1) + j * LANES == target, 1.0, 0.0).astype(jnp.bfloat16)
 
     picks = {}
-    for f in range(fields):
-        point = (lane + (LANES - f * half_step % LANES)) % LANES
-        for back in (0, 1):
-            p = half_step - 1 - point if back else point
-            p = jnp.clip(p, 0, half_step - 1)
-            low = p % 16
-            index = p - low + jnp.where(low < 8, 7 - low, low)
-            picks[f, back] = jnp.broadcast_to(index, (half_rows, LANES))
+    inner = lane % 64
+    for j in range(2):
+        for f in range(fields):
+            point = inner - f * quarter
+            point = (2 * j + lane // 64) * quarter + jnp.clip(point, 0, quarter - 1)
+            for back in (0, 1):
+                p = half_step - 1 - point if back else point
+                p = jnp.clip(p, 0, half_step - 1)
+                low = p % 16
+                index = p - low + jnp.where(low < 8, 7 - low, low)
+                picks[j, f, back] = jnp.broadcast_to(index, (half_rows, LANES))
     where_lane = iota((8, wide), 1)
     where_row = iota((8, wide), 0)
-    inside = jnp.where(where_lane < fields * half_step, where_lane % half_step, 1 << 20)
+    inner = where_lane % 64
+    inside = where_lane // 64 * quarter + inner % quarter
+    inside = jnp.where((inner < fields * quarter) & (inside < half_step), inside, 1 << 20)
     reach = {}
     for upper in (0, 1):
         i = where_row % 4 if upper else 3 - where_row % 4
         reach[upper] = (step * i + half_step * (where_row // 4) + inside).astype(jnp.float32)
+    half_lane = lane < 64
 
     for copy in wave_copies:
         copy.wait()
 
     copies = []
-    turn_sign = jnp.where(iota((8, 1), 0) < 4, -1.0, 1.0)
+    odd_row = iota((8, 1), 0) % 2
+    turn_sign = jnp.where(odd_row == 1, 1.0, -1.0)
     for r in range(cycles):
+        operands = ([], [])
         for t in range(tiles):
             at = slice(t * LANES, (t + 1) * LANES)
             coef = None
@@ -266,45 +293,45 @@
                     piece = pltpu.roll(piece, (to - start) % LANES, 1)
                 coef = piece if coef is None else jnp.where(lane >= to, piece, coef)
                 position += size
-            coef = coef * cen_ref[r, 0:1, at] + pltpu.roll(coef, 4, 0) * (cen_ref[r, 1:2, at] * turn_sign)
+            swapped = jnp.where(odd_row == 1, pltpu.roll(coef, 1, 0), pltpu.roll(coef, 7, 0))
+            coef = coef * cen_ref[r, 0:1, at] + swapped * (cen_ref[r, 1:2, at] * turn_sign)
             tc, ts = twist_ref[r, 0, :, at], twist_ref[r, 1, :, at]
-            for f in range(fields):
-                real, imag = coef[f : f + 1], coef[4 + f : 5 + f]
-                for which, first, value in ((0, 0, real * tc), (0, 1, imag * ts), (1, 0, real * ts), (1, 1, imag * tc)):
-                    high, low = split(value)
-                    base = (first * fields + f) * half_rows
-                    u_ref[which, base : base + half_rows, at] = high
-                    base += 2 * fields * half_rows
-                    u_ref[which, base : base + half_rows, at] = low
+            pairs = ([], [])
+            for first in (0, 1):
+                for f in range(fields):
+                    part = coef[2 * f + first : 2 * f + first + 1]
+                    for which in (0, 1):
+                        pairs[which].append(split(part * (tc if which == first else ts)))
+            for which in (0, 1):
+                operands[which].append(
+                    jnp.concatenate([high for high, _ in pairs[which]] + [low for _, low in pairs[which]], axis=0)
+                )
         both = []
         rows = 2 * fields * half_rows
         for which in (0, 1):
-            product = dot_nt(u_ref[which], tab_ref[r, which])
+            table = jnp.concatenate([tab_ref[r, which, t] for t in range(tiles)], axis=1)
+            product = dot_nt(jnp.concatenate(operands[which], axis=1), table)
             value = product[:rows] + product[rows:]
             both.append(value[:, :LANES] + jnp.concatenate([value[:, low_at:], jnp.zeros((rows, low_at - 16 * counts), jnp.float32)], axis=1))
         mixed = {}
         for f in range(fields):
             p1, p2 = (both[0][(i * fields + f) * half_rows : (i * fields + f + 1) * half_rows] for i in (0, 1))
             p3, p4 = (both[1][(i * fields + f) * half_rows : (i * fields + f + 1) * half_rows] for i in (0, 1))
-            even_up, odd_up = p1 - p2, p3 + p4
-            even_down, odd_down = p1 + p2, p4 - p3
-            for upper, even, odd in ((1, even_up, odd_up), (0, even_down, odd_down)):
+            for upper, even, odd in ((1, p1 - p2, p3 + p4), (0, p1 + p2, p4 - p3)):
                 for back, value in ((0, even - odd), (1, even + odd)):
-                    mixed[upper, back, f] = jnp.take_along_axis(
-                        value, picks[f, back], axis=1, mode="promise_in_bounds"
-                    )
+                    for j in range(2):
+                        mixed[upper, back, j, f] = jnp.take_along_axis(
+                            value, picks[j, f, back], axis=1, mode="promise_in_bounds"
+                        )
+        inner = lane % 64
         for upper in (0, 1):
             row_tiles = []
             for back in (1, 0):
                 pieces = []
-                for j in range(wide // LANES):
-                    piece = None
-                    for f in range(fields):
-                        start, stop = f * half_step - j * LANES, (f + 1) * half_step - j * LANES
-                        if stop <= 0 or start >= LANES:
-                            continue
-                        value = mixed[upper, back, f]
-                        piece = value if piece is None else jnp.where(lane >= start, value, piece)
+                for j in range(2):
+                    piece = mixed[upper, back, j, 0]
+                    for f in range(1, fields):
+                        piece = jnp.where(inner >= f * quarter, mixed[upper, back, j, f], piece)
                     pieces.append(piece)
                 row_tiles.append(jnp.concatenate(pieces, axis=1))
             for a in range(lev_count // 2):
@@ -331,22 +358,39 @@
         copies.append(started)
 
     upper = me >= lev_count // 2
-    sub = iota((8, place_ref.shape[1]), 0)
+    span = half_step * group
+    width = place_ref.shape[1]
+    sub = iota((8, width), 0)
     order = jnp.where(upper, sub, (sub // 4) * 4 + 3 - sub % 4)
+    spread_by = jnp.concatenate([place_ref[...], place_ref[...]], axis=0)
     for r in range(cycles):
         for copy in copies[r]:
             copy.wait()
-        high, low = split(got_ref[r].reshape(lev_count * 8, wide))
-        spread = jnp.dot(high, place_ref[...], preferred_element_type=jnp.float32) + jnp.dot(
-            low, place_ref[...], preferred_element_type=jnp.float32
-        )
-        total = spread[:8]
-        for level in range(1, lev_count):
-            total = total + pltpu.roll(spread[level * 8 : (level + 1) * 8], fields * level, 1)
-        total = jnp.take_along_axis(total, order, axis=0, mode="promise_in_bounds")
-        for q in range(8):
-            s = (q % 2) * 4 + q // 2
-            out_ref[r : r + 1, q * span : (q + 1) * span] = total[s : s + 1, :span]
+        rows = [[] for _ in range(4)]
+        for first in range(0, lev_count, 4):
+            for j in range(2):
+                at = slice(j * LANES, (j + 1) * LANES)
+                low_half, high_half = [], []
+                for level in (first, first + 2):
+                    one, two = got_ref[r, level, :, at], got_ref[r, level + 1, :, at]
+                    turned = pltpu.roll(jnp.where(half_lane, two, one), 64, 1)
+                    low_half.append(jnp.where(half_lane, one, turned))
+                    high_half.append(jnp.where(half_lane, turned, two))
+                rows[2 * j].append(jnp.concatenate(low_half, axis=1))
+                rows[2 * j + 1].append(jnp.concatenate(high_half, axis=1))
+        high, low = split(jnp.concatenate([row for quads in rows for row in quads], axis=0))
+        spread = jnp.dot(jnp.concatenate([high, low], axis=1), spread_by, preferred_element_type=jnp.float32)
+        sets = lev_count // 4
+        for q in range(4):
+            total = spread[8 * sets * q : 8 * sets * q + 8]
+            for i in range(1, sets):
+                total = total + pltpu.roll(spread[8 * (sets * q + i) : 8 * (sets * q + i) + 8], 4 * fields * i, 1)
+            total = jnp.take_along_axis(total, order, axis=0, mode="promise_in_bounds")
+            begin = q * quarter * group
+            size = min(quarter * group, span - begin)
+            for k in range(8):
+                s = (k % 2) * 4 + k // 2
+                out_ref[r : r + 1, k * span + begin : k * span + begin + size] = total[s : s + 1, :size]
 
 
 def local(spectral, legendre, slot_wave, cycle_len, lat_order):
@@ -363,13 +407,15 @@
     fields = parts // 2
     cycles = lat_order.shape[0] // wave_count
     groups = (slot_count + LANES - 1) // LANES
-    chunk = 32 if slot_count % 32 == 0 else 16
+    chunk = 64 if slot_count % 64 == 0 else BLOCK
     half_rows = 2 * lev_count
     counts = (half_step + 15) // 16
     low_at = (16 * counts + LANES - 1) // LANES * LANES
 
-    wide = (fields * half_step + LANES - 1) // LANES * LANES
-    span = (fields * lev_count * half_step + LANES - 1) // LANES * LANES
+    quarter = (half_step + 3) // 4
+    assert fields * quarter <= 64 and half_step <= LANES and lev_count % 4 == 0
+    wide = 2 * LANES
+    width = (quarter * fields * lev_count + LANES - 1) // LANES * LANES
     smem = pl.BlockSpec(memory_space=pltpu.SMEM)
     vmem = pl.BlockSpec(memory_space=pltpu.VMEM)
     hbm = pl.BlockSpec(memory_space=pl.ANY)
@@ -387,9 +433,8 @@
             pltpu.VMEM((groups, wave_count, cycles, 8, LANES), jnp.float32),
             pltpu.VMEM((cycles, 2, half_rows, slots), jnp.float32),
             pltpu.VMEM((cycles, 8, slots), jnp.float32),
-            pltpu.VMEM((cycles, 2, low_at + 16 * counts, slots), jnp.bfloat16),
-            pltpu.VMEM((2, 4 * fields * half_rows, slots), jnp.bfloat16),
-            pltpu.VMEM((wide, span), jnp.bfloat16),
+            pltpu.VMEM((cycles, 2, slots // LANES, low_at + 16 * counts, LANES), jnp.bfloat16),
+            pltpu.VMEM((2 * LANES, width), jnp.bfloat16),
             pltpu.VMEM((cycles, lev_count, 8, wide), jnp.float32),
             pltpu.VMEM((cycles, lev_count, 8, wide), jnp.float32),
             pltpu.SemaphoreType.DMA((2, slot_count // chunk)),

time: 24 us -> 23.3 us (0.971)
  Pallas kernels: 23.1 us -> 22.4 us
    pallas_call x1, Pallas kernels: 23.1 us -> 22.4 us  [local(): pl.pallas_call(functools.partial(kernel, half_step, chunk), out_shape=plt...]
where the time goes in v2:
time: 23.3 us; the launch traced here: 23.1 us
  Pallas kernels  22.4 us (96%)
  local copies, waits for them, and re-layouts  0.7 us (3%)
    pallas_call x1, Pallas kernels, local(): pl.pallas_call(functools.partial(kernel, half_step, chunk), out_shape=plt...  22.4 us
    unnamed x1, local copies, waits for them, and re-layouts  0.7 us

profile of v2, /device:TPU:0, one launch (start us, length us, event | category | flops | bytes accessed | tf_op | source)
XLA Modules:
  0.0 23.1 jit_solution(3333562190089522323)
XLA Ops:
  0.0 22.4 %transform.1 = f32[3,15552]{1,0:T(4,128)S(1)} custom-call(s32[1280]{0:T(1024)} %wave_ref.1, s32[12]{0:T(128)} %lat_ref.1, s32[6]{0:T(128)} %cycle_ref.1, bf16[6,320,1280]{2,1,0:T(8,128)(2,1)} %bitcast.2, bf16[6,320,1280]{2,1,0:T(8,128)(2,1)} %bitcast.3), custom_call_target="tpu_custom_call" | custom-call | tf_op jit(solution)/shard_map/transform/pallas_call | solution.py:422
  22.4 0.7 %copy.7 = f32[3,15552]{1,0:T(4,128)} copy(f32[3,15552]{1,0:T(4,128)S(1)} %transform.1) | data formatting | bytes 373248

commit v3 on v2

--- a/solution.py
+++ b/solution.py
@@ -11,6 +11,7 @@
 RMAX = 5136
 LANES = 128
 BLOCK = 16
+AHEAD = 3
 
 
 def split(value):
@@ -42,11 +43,12 @@
 
 
 def kernel(
-    half_step, chunk,
-    wave_ref, lat_ref, cycle_ref, spec_hbm, leg_hbm, out_ref,
+    half_step, chunks,
+    wave_hbm, lat_hbm, cycle_hbm, spec_hbm, leg_hbm, out_ref,
+    wave_ref, lat_ref, cycle_ref,
     spec_ref, leg_ref, col_ref, four_ref, wsend_ref, wgot_ref,
     twist_ref, cen_ref, tab_ref, place_ref, send_ref, got_ref,
-    load_sem, wown_sem, wsend_sem, wrecv_sem, own_sem, send_sem, recv_sem,
+    small_sem, load_sem, wown_sem, wsend_sem, wrecv_sem, own_sem, send_sem, recv_sem,
 ):
     parts, slot_count, degrees = spec_ref.shape
     half_cycles = leg_ref.shape[0]
@@ -66,6 +68,25 @@
     my_wave = lax.axis_index("wave")
     first_row = my_wave * cycles
 
+    loads, starts = [], []
+    start = 0
+    for i, size in enumerate(chunks):
+        at = pl.ds(start, size)
+        loads.append([
+            pltpu.make_async_copy(leg_hbm.at[:, at], leg_ref.at[:, at], load_sem.at[0, i]),
+            pltpu.make_async_copy(spec_hbm.at[:, at], spec_ref.at[:, at], load_sem.at[1, i]),
+        ])
+        starts.append(start)
+        start += size
+    small = [
+        pltpu.make_async_copy(source, target, small_sem.at[i])
+        for i, (source, target) in enumerate(((wave_hbm, wave_ref), (lat_hbm, lat_ref), (cycle_hbm, cycle_ref)))
+    ]
+    for copy in small:
+        copy.start()
+    for pair in loads[:AHEAD]:
+        for copy in pair:
+            copy.start()
     barrier = pltpu.get_barrier_semaphore()
     for offset in range(1, lev_count):
         peer = lax.rem(me + offset, lev_count)
@@ -73,17 +94,8 @@
     for offset in range(1, wave_count):
         peer = lax.rem(my_wave + offset, wave_count)
         pl.semaphore_signal(barrier, inc=1, device_id={"wave": peer}, device_id_type=pl.DeviceIdType.MESH)
-
-    loads = []
-    for i in range(slot_count // chunk):
-        at = pl.ds(i * chunk, chunk)
-        pair = [
-            pltpu.make_async_copy(leg_hbm.at[:, at], leg_ref.at[:, at], load_sem.at[0, i]),
-            pltpu.make_async_copy(spec_hbm.at[:, at], spec_ref.at[:, at], load_sem.at[1, i]),
-        ]
-        for copy in pair:
-            copy.start()
-        loads.append(pair)
+    for copy in small:
+        copy.wait()
 
     waves = wave_ref[...].reshape(1, slots).astype(jnp.float32)
 
@@ -144,24 +156,24 @@
                 tab_ref[r, which, t, 16 * k : 16 * k + 16, :] = high
                 tab_ref[r, which, t, low_at + 16 * k : low_at + 16 * k + 16, :] = low
 
-    chunks = LANES // BLOCK
+    turns_count = LANES // BLOCK
     lane = iota((1, LANES), 1)
     lane_chunk = lane // BLOCK
-    flip = jnp.where((iota((BLOCK, degrees), 1) & 1) == 1, -1.0, 1.0).astype(jnp.bfloat16)
+    flip = jnp.where((iota((BLOCK, LANES), 1) & 1) == 1, -1.0, 1.0).astype(jnp.bfloat16)
     lats = 2 * half_cycles
     own = iota((BLOCK, lats * BLOCK), 0) == iota((BLOCK, lats * BLOCK), 1) % BLOCK
 
     def legendre(b, turn):
         at = slice(b * BLOCK, (b + 1) * BLOCK)
         column = col_ref[at, :]
-        live = jnp.concatenate(
-            [jnp.where(column <= float(d), 1.0, 0.0) for d in range(0, degrees, LANES)], axis=1
-        ).astype(jnp.bfloat16)
-        north = leg_ref[:, at, :] * live[None]
-        south = north * flip[None]
-        both = (north, south)
         order = [(j - turn) % lats for j in range(lats)]
-        table = jnp.concatenate([both[j // half_cycles][j % half_cycles] for j in order], axis=0)
+        columns = []
+        for d in range(0, degrees, LANES):
+            live = jnp.where(column <= float(d), 1.0, 0.0).astype(jnp.bfloat16)
+            north = [live * leg_ref[k, at, d : d + LANES] for k in range(half_cycles)]
+            both = north + [flip * value for value in north]
+            columns.append(jnp.concatenate([both[j] for j in order], axis=0))
+        table = jnp.concatenate(columns, axis=1)
         product = dot_nt(spec_ref[:, at, :].reshape(parts * BLOCK, degrees), table)
         product = product.reshape(parts, BLOCK, lats * BLOCK)
         total = jnp.sum(jnp.where(own[None], product, 0.0), axis=1)
@@ -178,7 +190,9 @@
             shifts = {}
             for b, total in enumerate(sums):
                 place = (j + b) % lats
-                shifts.setdefault((b - place) % chunks, []).append((b, place % chunks, total[place // chunks]))
+                shifts.setdefault((b - place) % turns_count, []).append(
+                    (b, place % turns_count, total[place // turns_count])
+                )
             value = None
             for shift, members in shifts.items():
                 picked = None
@@ -217,25 +231,21 @@
 
     for t in range(tiles):
         tables(0, t)
-    ahead = [(r, t) for r in range(1, min(2, cycles)) for t in range(tiles)]
     total_blocks = slot_count // BLOCK
-    done = 0
     sums = []
     for b in range(total_blocks):
-        if b * BLOCK % chunk == 0:
-            for copy in loads[b * BLOCK // chunk]:
+        if b * BLOCK in starts:
+            i = starts.index(b * BLOCK)
+            for copy in loads[i]:
                 copy.wait()
-        sums.append(legendre(b, b % chunks))
-        upto = len(ahead) * (b + 1) // total_blocks
-        for r, t in ahead[done:upto]:
-            tables(r, t)
-        done = upto
-        if b % chunks == chunks - 1 or b == total_blocks - 1:
-            send_group(b // chunks, sums)
+            for copy in loads[i + AHEAD] if i + AHEAD < len(loads) else ():
+                copy.start()
+        sums.append(legendre(b, b % turns_count))
+        if b % turns_count == turns_count - 1 or b == total_blocks - 1:
+            send_group(b // turns_count, sums)
             sums = []
-    for r in range(2, cycles):
-        for t in range(tiles):
-            tables(r, t)
+    for t in range(tiles if cycles > 1 else 0):
+        tables(1, t)
 
     group = lev_count * fields
     quarter = (half_step + 3) // 4
@@ -278,6 +288,8 @@
     odd_row = iota((8, 1), 0) % 2
     turn_sign = jnp.where(odd_row == 1, 1.0, -1.0)
     for r in range(cycles):
+        for t in range(tiles if r > 1 else 0):
+            tables(r, t)
         operands = ([], [])
         for t in range(tiles):
             at = slice(t * LANES, (t + 1) * LANES)
@@ -339,9 +351,9 @@
                 tile = jnp.concatenate([value[4 * a : 4 * a + 4] for value in row_tiles], axis=0)
                 send_ref[r, dest] = jnp.where(reach[upper] < lengths[r] - float(points_dev * dest), tile, 0.0)
         started = []
-        offsets = sorted(range(1, lev_count), key=lambda o: abs(o - lev_count / 2))
-        for offset in offsets:
-            peer = lax.rem(me + offset, lev_count)
+        paired = lev_count & (lev_count - 1) == 0
+        for offset in range(lev_count - 1, 0, -1):
+            peer = me ^ offset if paired else lax.rem(me + offset, lev_count)
             copy = pltpu.make_async_remote_copy(
                 src_ref=send_ref.at[r, peer],
                 dst_ref=got_ref.at[r, me],
@@ -407,7 +419,11 @@
     fields = parts // 2
     cycles = lat_order.shape[0] // wave_count
     groups = (slot_count + LANES - 1) // LANES
-    chunk = 64 if slot_count % 64 == 0 else BLOCK
+    chunks, left = [], slot_count
+    while left:
+        size = 64 if left > 64 else min(left, 32)
+        chunks.append(size)
+        left -= size
     half_rows = 2 * lev_count
     counts = (half_step + 15) // 16
     low_at = (16 * counts + LANES - 1) // LANES * LANES
@@ -416,15 +432,17 @@
     assert fields * quarter <= 64 and half_step <= LANES and lev_count % 4 == 0
     wide = 2 * LANES
     width = (quarter * fields * lev_count + LANES - 1) // LANES * LANES
-    smem = pl.BlockSpec(memory_space=pltpu.SMEM)
     vmem = pl.BlockSpec(memory_space=pltpu.VMEM)
     hbm = pl.BlockSpec(memory_space=pl.ANY)
     return pl.pallas_call(
-        functools.partial(kernel, half_step, chunk),
+        functools.partial(kernel, half_step, tuple(chunks)),
         out_shape=pltpu.VMEM((cycles, points_dev * lev_count * fields), jnp.float32),
-        in_specs=[vmem, smem, smem, hbm, hbm],
+        in_specs=[hbm] * 5,
         out_specs=vmem,
         scratch_shapes=[
+            pltpu.VMEM(slot_wave.shape, jnp.int32),
+            pltpu.SMEM(lat_order.shape, jnp.int32),
+            pltpu.SMEM(cycle_len.shape, jnp.int32),
             pltpu.VMEM((parts, slot_count, degrees), jnp.bfloat16),
             pltpu.VMEM((half_cycles, slot_count, degrees), jnp.bfloat16),
             pltpu.VMEM((groups * LANES, LANES), jnp.float32),
@@ -437,7 +455,8 @@
             pltpu.VMEM((2 * LANES, width), jnp.bfloat16),
             pltpu.VMEM((cycles, lev_count, 8, wide), jnp.float32),
             pltpu.VMEM((cycles, lev_count, 8, wide), jnp.float32),
-            pltpu.SemaphoreType.DMA((2, slot_count // chunk)),
+            pltpu.SemaphoreType.DMA((3,)),
+            pltpu.SemaphoreType.DMA((2, len(chunks))),
             pltpu.SemaphoreType.DMA((groups,)),
             pltpu.SemaphoreType.DMA((groups, wave_count)),
             pltpu.SemaphoreType.DMA((groups, wave_count)),

time: 23.3 us -> 22.9 us (0.983)
  Pallas kernels: 22.4 us -> 22.1 us
    pallas_call x1, Pallas kernels: 22.4 us -> 22.1 us  [local(): pl.pallas_call(functools.partial(kernel, half_step, tuple(chunks)), out_s...]
where the time goes in v3:
time: 22.9 us; the launch traced here: 22.8 us
  Pallas kernels  22.1 us (97%)
  local copies, waits for them, and re-layouts  0.7 us (3%)
    pallas_call x1, Pallas kernels, local(): pl.pallas_call(functools.partial(kernel, half_step, tuple(chunks)), out_s...  22.1 us
    unnamed x1, local copies, waits for them, and re-layouts  0.7 us

profile of v3, /device:TPU:0, one launch (start us, length us, event | category | flops | bytes accessed | tf_op | source)
XLA Modules:
  0.0 22.8 jit_solution(16700937810157787096)
XLA Ops:
  0.0 22.1 %transform.1 = f32[3,15552]{1,0:T(4,128)S(1)} custom-call(s32[1280]{0:T(1024)} %wave_hbm.1, s32[12]{0:T(128)} %lat_hbm.1, s32[6]{0:T(128)} %cycle_hbm.1, bf16[6,320,1280]{2,1,0:T(8,128)(2,1)} %bitcast.2, bf16[6,320,1280]{2,1,0:T(8,128)(2,1)} %bitcast.3), custom_call_target="tpu_custom_call" | custom-call | tf_op jit(solution)/shard_map/transform/pallas_call | solution.py:437
  22.1 0.7 %copy.7 = f32[3,15552]{1,0:T(4,128)} copy(f32[3,15552]{1,0:T(4,128)S(1)} %transform.1) | data formatting | bytes 373248

commit v4 on v3

--- a/solution.py
+++ b/solution.py
@@ -161,53 +161,50 @@
     lane_chunk = lane // BLOCK
     flip = jnp.where((iota((BLOCK, LANES), 1) & 1) == 1, -1.0, 1.0).astype(jnp.bfloat16)
     lats = 2 * half_cycles
-    own = iota((BLOCK, lats * BLOCK), 0) == iota((BLOCK, lats * BLOCK), 1) % BLOCK
-
-    def legendre(b, turn):
+    own = iota((BLOCK, parts * BLOCK), 0) == iota((BLOCK, parts * BLOCK), 1) % BLOCK
+    south_row = iota((lats, 1), 0) >= half_cycles
+
+    def legendre(b):
         at = slice(b * BLOCK, (b + 1) * BLOCK)
         column = col_ref[at, :]
-        order = [(j - turn) % lats for j in range(lats)]
         columns = []
         for d in range(0, degrees, LANES):
             live = jnp.where(column <= float(d), 1.0, 0.0).astype(jnp.bfloat16)
             north = [live * leg_ref[k, at, d : d + LANES] for k in range(half_cycles)]
-            both = north + [flip * value for value in north]
-            columns.append(jnp.concatenate([both[j] for j in order], axis=0))
-        table = jnp.concatenate(columns, axis=1)
-        product = dot_nt(spec_ref[:, at, :].reshape(parts * BLOCK, degrees), table)
-        product = product.reshape(parts, BLOCK, lats * BLOCK)
+            columns.append(jnp.concatenate(north + [flip * value for value in north], axis=0))
+        rows = jnp.concatenate([spec_ref[(j - b) % parts, at, :] for j in range(parts)], axis=0)
+        return dot_nt(jnp.concatenate(columns, axis=1), rows)
+
+    def diagonal(product):
+        product = product.reshape(lats, BLOCK, parts * BLOCK)
         total = jnp.sum(jnp.where(own[None], product, 0.0), axis=1)
-        extra = -total.shape[1] % LANES
-        if extra:
-            total = jnp.concatenate([total, jnp.zeros((parts, extra), jnp.float32)], axis=1)
-        return [total[:, j * LANES : (j + 1) * LANES] for j in range(total.shape[1] // LANES)]
+        return jnp.concatenate([total, jnp.zeros((lats, LANES - parts * BLOCK), jnp.float32)], axis=1)
 
     wave_copies = []
 
     def send_group(g, sums):
-        sign = jnp.where((mine[:, g * LANES : (g + 1) * LANES].astype(jnp.int32) & 1) == 1, -1.0, 1.0)
-        for j in range(lats):
+        odd = (mine[:, g * LANES : (g + 1) * LANES].astype(jnp.int32) & 1) == 1
+        sign = jnp.where(south_row & odd, -1.0, 1.0)
+        for c in range(parts):
             shifts = {}
-            for b, total in enumerate(sums):
-                place = (j + b) % lats
-                shifts.setdefault((b - place) % turns_count, []).append(
-                    (b, place % turns_count, total[place // turns_count])
-                )
+            for i, (b, total) in enumerate(sums):
+                place = (c + b) % parts
+                shifts.setdefault((i - place) % turns_count, []).append((i, place, total))
             value = None
             for shift, members in shifts.items():
                 picked = None
-                for b, at_chunk, total in members:
-                    picked = total if picked is None else jnp.where(lane_chunk == at_chunk, total, picked)
+                for i, place, total in members:
+                    picked = total if picked is None else jnp.where(lane_chunk == place, total, picked)
                 if shift:
                     picked = pltpu.roll(picked, shift * BLOCK, 1)
-                first, last = members[0][0], members[-1][0]
                 if value is None:
                     value = picked
                 else:
-                    value = jnp.where((lane_chunk >= first) & (lane_chunk <= last), picked, value)
-            if j >= half_cycles:
-                value = value * sign
-            four_ref[j, 0:parts, :] = value
+                    mask = lane_chunk == members[0][0]
+                    for i, _, _ in members[1:]:
+                        mask = mask | (lane_chunk == i)
+                    value = jnp.where(mask, picked, value)
+            four_ref[:, c, :] = value * sign
         for w in range(wave_count):
             for r in range(cycles):
                 wsend_ref[g, w, r] = four_ref[lat_ref[w * cycles + r]]
@@ -229,10 +226,20 @@
         kept.start()
         wave_copies.append(kept)
 
-    for t in range(tiles):
-        tables(0, t)
+    early = min(2, cycles)
+    for r in range(early):
+        for t in range(tiles):
+            tables(r, t)
     total_blocks = slot_count // BLOCK
     sums = []
+
+    def finish(b, product):
+        sums.append((b, diagonal(product)))
+        if b % turns_count == turns_count - 1 or b == total_blocks - 1:
+            send_group(b // turns_count, sums)
+            sums.clear()
+
+    pending = None
     for b in range(total_blocks):
         if b * BLOCK in starts:
             i = starts.index(b * BLOCK)
@@ -240,12 +247,14 @@
                 copy.wait()
             for copy in loads[i + AHEAD] if i + AHEAD < len(loads) else ():
                 copy.start()
-        sums.append(legendre(b, b % turns_count))
-        if b % turns_count == turns_count - 1 or b == total_blocks - 1:
-            send_group(b // turns_count, sums)
-            sums = []
-    for t in range(tiles if cycles > 1 else 0):
-        tables(1, t)
+        product = legendre(b)
+        if pending is not None:
+            finish(*pending)
+        pending = (b, product)
+    finish(*pending)
+    for r in range(early, cycles):
+        for t in range(tiles):
+            tables(r, t)
 
     group = lev_count * fields
     quarter = (half_step + 3) // 4
@@ -288,8 +297,6 @@
     odd_row = iota((8, 1), 0) % 2
     turn_sign = jnp.where(odd_row == 1, 1.0, -1.0)
     for r in range(cycles):
-        for t in range(tiles if r > 1 else 0):
-            tables(r, t)
         operands = ([], [])
         for t in range(tiles):
             at = slice(t * LANES, (t + 1) * LANES)
@@ -421,7 +428,7 @@
     groups = (slot_count + LANES - 1) // LANES
     chunks, left = [], slot_count
     while left:
-        size = 64 if left > 64 else min(left, 32)
+        size = 64 if 64 < left < slot_count else min(left, 32)
         chunks.append(size)
         left -= size
     half_rows = 2 * lev_count

time: 22.9 us -> 23 us (level)
  no operation moved by 1% of the time
where the time goes in v4:
time: 23 us; the launch traced here: 22.9 us
  Pallas kernels  22.2 us (97%)
  local copies, waits for them, and re-layouts  0.7 us (3%)
    pallas_call x1, Pallas kernels, local(): pl.pallas_call(functools.partial(kernel, half_step, tuple(chunks)), out_s...  22.2 us
    unnamed x1, local copies, waits for them, and re-layouts  0.7 us

profile of v4, /device:TPU:0, one launch (start us, length us, event | category | flops | bytes accessed | tf_op | source)
XLA Modules:
  0.0 22.9 jit_solution(1002255304489114911)
XLA Ops:
  0.0 22.2 %transform.1 = f32[3,15552]{1,0:T(4,128)S(1)} custom-call(s32[1280]{0:T(1024)} %wave_hbm.1, s32[12]{0:T(128)} %lat_hbm.1, s32[6]{0:T(128)} %cycle_hbm.1, bf16[6,320,1280]{2,1,0:T(8,128)(2,1)} %bitcast.2, bf16[6,320,1280]{2,1,0:T(8,128)(2,1)} %bitcast.3), custom_call_target="tpu_custom_call" | custom-call | tf_op jit(solution)/shard_map/transform/pallas_call | solution.py:444
  22.2 0.7 %copy.7 = f32[3,15552]{1,0:T(4,128)} copy(f32[3,15552]{1,0:T(4,128)S(1)} %transform.1) | data formatting | bytes 373248

commit v5 on v4

--- a/solution.py
+++ b/solution.py
@@ -46,21 +46,23 @@
     half_step, chunks,
     wave_hbm, lat_hbm, cycle_hbm, spec_hbm, leg_hbm, out_ref,
     wave_ref, lat_ref, cycle_ref,
-    spec_ref, leg_ref, col_ref, four_ref, wsend_ref, wgot_ref,
+    spec_ref, leg_ref, col_ref, four_ref, wsend_ref, wgot_ref, wsend_last_ref, wgot_last_ref,
     twist_ref, cen_ref, tab_ref, place_ref, send_ref, got_ref,
     small_sem, load_sem, wown_sem, wsend_sem, wrecv_sem, own_sem, send_sem, recv_sem,
 ):
     parts, slot_count, degrees = spec_ref.shape
     half_cycles = leg_ref.shape[0]
     fields = parts // 2
-    groups, wave_count, cycles = wsend_ref.shape[:3]
+    wave_count, cycles = wsend_ref.shape[1:3]
+    groups = (slot_count + LANES - 1) // LANES
+    packed = 0 < slot_count % LANES <= LANES // 2
     lev_count = send_ref.shape[1]
     wide = send_ref.shape[-1]
     slots = wave_ref.shape[0]
     tiles = slots // LANES
     step = 2 * half_step
     points_dev = 4 * step
-    half_rows = twist_ref.shape[2]
+    half_rows = twist_ref.shape[3]
     blocks = half_rows // 8
     counts = (half_step + 15) // 16
     low_at = tab_ref.shape[3] - 16 * counts
@@ -134,17 +136,17 @@
         cosine, sine = turns((phase - whole * length) * inverse)
         nc, ns, tc, ts = cosine[0:8], sine[0:8], cosine[8:16], sine[8:16]
         rc, rs = cosine[16:], sine[16:]
-        twist_ref[r, 0, 0:8, at] = tc
-        twist_ref[r, 1, 0:8, at] = ts
+        twist_ref[r, 0, t, 0:8, :] = tc
+        twist_ref[r, 1, t, 0:8, :] = ts
         for a in range(1, blocks):
             i = counts + a - 1
             c, s = rc[i : i + 1], rs[i : i + 1]
-            twist_ref[r, 0, 8 * a : 8 * a + 8, at] = tc * c - ts * s
-            twist_ref[r, 1, 8 * a : 8 * a + 8, at] = ts * c + tc * s
+            twist_ref[r, 0, t, 8 * a : 8 * a + 8, :] = tc * c - ts * s
+            twist_ref[r, 1, t, 8 * a : 8 * a + 8, :] = ts * c + tc * s
         weight = jnp.where(wave == 0.0, 1.0, 2.0)
         i = rest_count - 1
-        cen_ref[r, 0:1, at] = rc[i : i + 1] * weight
-        cen_ref[r, 1:2, at] = rs[i : i + 1] * weight
+        cen_ref[r, t, 0:1, :] = rc[i : i + 1] * weight
+        cen_ref[r, t, 1:2, :] = rs[i : i + 1] * weight
         for k in range(counts):
             c, s = rc[k : k + 1], rs[k : k + 1]
             cc, ss, sc, cs = c * nc, s * ns, s * nc, c * ns
@@ -180,16 +182,24 @@
         total = jnp.sum(jnp.where(own[None], product, 0.0), axis=1)
         return jnp.concatenate([total, jnp.zeros((lats, LANES - parts * BLOCK), jnp.float32)], axis=1)
 
-    wave_copies = []
+    wave_paired = wave_count & (wave_count - 1) == 0
+    halves = 2 if wave_count == 4 and 2 * slot_count % LANES == 0 else 1
+    near = (1,) if halves == 2 else tuple(range(wave_count))
+    wave_copies = {False: [], True: []}
 
     def send_group(g, sums):
-        odd = (mine[:, g * LANES : (g + 1) * LANES].astype(jnp.int32) & 1) == 1
-        sign = jnp.where(south_row & odd, -1.0, 1.0)
+        pack = packed and g == groups - 1
+        number = mine[:, g * LANES : (g + 1) * LANES]
+        if pack:
+            number = jnp.where(lane < LANES // 2, number, pltpu.roll(number, LANES // 2, 1))
+        sign = jnp.where(south_row & ((number.astype(jnp.int32) & 1) == 1), -1.0, 1.0)
+        values = []
         for c in range(parts):
+            move = turns_count // 2 if pack and c % 2 else 0
             shifts = {}
             for i, (b, total) in enumerate(sums):
                 place = (c + b) % parts
-                shifts.setdefault((i - place) % turns_count, []).append((i, place, total))
+                shifts.setdefault((i + move - place) % turns_count, []).append((i + move, place, total))
             value = None
             for shift, members in shifts.items():
                 picked = None
@@ -204,27 +214,39 @@
                     for i, _, _ in members[1:]:
                         mask = mask | (lane_chunk == i)
                     value = jnp.where(mask, picked, value)
-            four_ref[:, c, :] = value * sign
+            values.append(value)
+        if pack:
+            for f in range(fields):
+                four_ref[:, f, :] = jnp.where(lane < LANES // 2, values[2 * f], values[2 * f + 1]) * sign
+        else:
+            for c in range(parts):
+                four_ref[:, (c % 2) * 4 + c // 2, :] = values[c] * sign
         for w in range(wave_count):
             for r in range(cycles):
-                wsend_ref[g, w, r] = four_ref[lat_ref[w * cycles + r]]
+                lat = lat_ref[w * cycles + r]
+                if pack:
+                    wsend_last_ref[w, r] = four_ref[lat, 0:4, :]
+                else:
+                    wsend_ref[g, w, r] = four_ref[lat]
+        source = wsend_last_ref if pack else wsend_ref.at[g]
+        target = wgot_last_ref if pack else wgot_ref.at[g]
         if g == 0:
             pl.semaphore_wait(barrier, lev_count + wave_count - 2)
-        for offset in range(1, wave_count):
-            peer = lax.rem(my_wave + offset, wave_count)
+        for offset in range(wave_count - 1, 0, -1):
+            peer = my_wave ^ offset if wave_paired else lax.rem(my_wave + offset, wave_count)
             copy = pltpu.make_async_remote_copy(
-                src_ref=wsend_ref.at[g, peer],
-                dst_ref=wgot_ref.at[g, my_wave],
+                src_ref=source.at[peer],
+                dst_ref=target.at[my_wave],
                 send_sem=wsend_sem.at[g, offset],
                 recv_sem=wrecv_sem.at[g, offset],
                 device_id={"wave": peer},
                 device_id_type=pl.DeviceIdType.MESH,
             )
             copy.start()
-            wave_copies.append(copy)
-        kept = pltpu.make_async_copy(wsend_ref.at[g, my_wave], wgot_ref.at[g, my_wave], wown_sem.at[g])
+            wave_copies[offset in near].append(copy)
+        kept = pltpu.make_async_copy(source.at[my_wave], target.at[my_wave], wown_sem.at[g])
         kept.start()
-        wave_copies.append(kept)
+        wave_copies[1].append(kept)
 
     early = min(2, cycles)
     for r in range(early):
@@ -290,48 +312,70 @@
         reach[upper] = (step * i + half_step * (where_row // 4) + inside).astype(jnp.float32)
     half_lane = lane < 64
 
-    for copy in wave_copies:
-        copy.wait()
-
     copies = []
-    odd_row = iota((8, 1), 0) % 2
-    turn_sign = jnp.where(odd_row == 1, 1.0, -1.0)
-    for r in range(cycles):
-        operands = ([], [])
-        for t in range(tiles):
-            at = slice(t * LANES, (t + 1) * LANES)
+    turn_sign = jnp.where(iota((8, 1), 0) < 4, -1.0, 1.0)
+    half_tiles = tiles // halves
+    half_waves = wave_count // halves
+    rows = 2 * fields * half_rows
+
+    def transform(r, h):
+        side = (my_wave // half_waves) ^ h if halves == 2 else 0
+        operands, tabs = ([], []), ([], [])
+        for tt in range(half_tiles):
+            t = side * half_tiles + tt
             coef = None
-            position = t * LANES
-            while position < (t + 1) * LANES:
-                w, inner = position // slot_count, position % slot_count
+            position = tt * LANES
+            while position < (tt + 1) * LANES:
+                w, inner = side * half_waves + position // slot_count, position % slot_count
                 g, start = inner // LANES, inner % LANES
-                size = min((t + 1) * LANES - position, slot_count - inner, LANES - start)
-                piece = wgot_ref[g, w, r]
-                to = position - t * LANES
+                size = min((tt + 1) * LANES - position, slot_count - inner, LANES - start)
+                if packed and g == groups - 1:
+                    piece = wgot_last_ref[w, r]
+                    piece = jnp.concatenate([piece, pltpu.roll(piece, LANES // 2, 1)], axis=0)
+                else:
+                    piece = wgot_ref[g, w, r]
+                to = position - tt * LANES
                 if to != start:
                     piece = pltpu.roll(piece, (to - start) % LANES, 1)
                 coef = piece if coef is None else jnp.where(lane >= to, piece, coef)
                 position += size
-            swapped = jnp.where(odd_row == 1, pltpu.roll(coef, 1, 0), pltpu.roll(coef, 7, 0))
-            coef = coef * cen_ref[r, 0:1, at] + swapped * (cen_ref[r, 1:2, at] * turn_sign)
-            tc, ts = twist_ref[r, 0, :, at], twist_ref[r, 1, :, at]
+            coef = coef * cen_ref[r, t, 0:1, :] + pltpu.roll(coef, 4, 0) * (cen_ref[r, t, 1:2, :] * turn_sign)
+            tc, ts = twist_ref[r, 0, t], twist_ref[r, 1, t]
             pairs = ([], [])
             for first in (0, 1):
                 for f in range(fields):
-                    part = coef[2 * f + first : 2 * f + first + 1]
+                    part = coef[4 * first + f : 4 * first + f + 1]
                     for which in (0, 1):
                         pairs[which].append(split(part * (tc if which == first else ts)))
             for which in (0, 1):
                 operands[which].append(
                     jnp.concatenate([high for high, _ in pairs[which]] + [low for _, low in pairs[which]], axis=0)
                 )
+                tabs[which].append(tab_ref[r, which, t])
         both = []
-        rows = 2 * fields * half_rows
         for which in (0, 1):
-            table = jnp.concatenate([tab_ref[r, which, t] for t in range(tiles)], axis=1)
-            product = dot_nt(jnp.concatenate(operands[which], axis=1), table)
-            value = product[:rows] + product[rows:]
-            both.append(value[:, :LANES] + jnp.concatenate([value[:, low_at:], jnp.zeros((rows, low_at - 16 * counts), jnp.float32)], axis=1))
+            product = dot_nt(jnp.concatenate(operands[which], axis=1), jnp.concatenate(tabs[which], axis=1))
+            both.append(product[:rows] + product[rows:])
+        return both
+
+    for copy in wave_copies[True]:
+        copy.wait()
+    if halves == 2:
+        begun = transform(0, 0)
+    for copy in wave_copies[False]:
+        copy.wait()
+
+    for r in range(cycles):
+        if halves == 2:
+            first = begun if r == 0 else transform(r, 0)
+            value = [one + two for one, two in zip(first, transform(r, 1))]
+        else:
+            value = transform(r, 0)
+        both = [
+            one[:, :LANES]
+            + jnp.concatenate([one[:, low_at:], jnp.zeros((rows, low_at - 16 * counts), jnp.float32)], axis=1)
+            for one in value
+        ]
         mixed = {}
         for f in range(fields):
             p1, p2 = (both[0][(i * fields + f) * half_rows : (i * fields + f + 1) * half_rows] for i in (0, 1))
@@ -431,6 +475,7 @@
         size = 64 if 64 < left < slot_count else min(left, 32)
         chunks.append(size)
         left -= size
+    packed = 0 < slot_count % LANES <= LANES // 2
     half_rows = 2 * lev_count
     counts = (half_step + 15) // 16
     low_at = (16 * counts + LANES - 1) // LANES * LANES
@@ -454,10 +499,12 @@
             pltpu.VMEM((half_cycles, slot_count, degrees), jnp.bfloat16),
             pltpu.VMEM((groups * LANES, LANES), jnp.float32),
             pltpu.VMEM((2 * half_cycles, 8, LANES), jnp.float32),
-            pltpu.VMEM((groups, wave_count, cycles, 8, LANES), jnp.float32),
-            pltpu.VMEM((groups, wave_count, cycles, 8, LANES), jnp.float32),
-            pltpu.VMEM((cycles, 2, half_rows, slots), jnp.float32),
-            pltpu.VMEM((cycles, 8, slots), jnp.float32),
+            pltpu.VMEM((max(1, groups - packed), wave_count, cycles, 8, LANES), jnp.float32),
+            pltpu.VMEM((max(1, groups - packed), wave_count, cycles, 8, LANES), jnp.float32),
+            pltpu.VMEM((wave_count, cycles, 4, LANES), jnp.float32),
+            pltpu.VMEM((wave_count, cycles, 4, LANES), jnp.float32),
+            pltpu.VMEM((cycles, 2, slots // LANES, half_rows, LANES), jnp.float32),
+            pltpu.VMEM((cycles, slots // LANES, 8, LANES), jnp.float32),
             pltpu.VMEM((cycles, 2, slots // LANES, low_at + 16 * counts, LANES), jnp.bfloat16),
             pltpu.VMEM((2 * LANES, width), jnp.bfloat16),
             pltpu.VMEM((cycles, lev_count, 8, wide), jnp.float32),

time: 23 us -> 22.8 us (level)
  Pallas kernels: 22.2 us -> 21.9 us
    pallas_call x1, Pallas kernels: 22.2 us -> 21.9 us  [local(): pl.pallas_call(functools.partial(kernel, half_step, tuple(chunks)), out_s...]
where the time goes in v5:
time: 22.8 us; the launch traced here: 22.6 us
  Pallas kernels  21.9 us (96%)
  local copies, waits for them, and re-layouts  0.7 us (3%)
    pallas_call x1, Pallas kernels, local(): pl.pallas_call(functools.partial(kernel, half_step, tuple(chunks)), out_s...  21.9 us
    unnamed x1, local copies, waits for them, and re-layouts  0.7 us

profile of v5, /device:TPU:0, one launch (start us, length us, event | category | flops | bytes accessed | tf_op | source)
XLA Modules:
  0.0 22.6 jit_solution(8549432944920250017)
XLA Ops:
  0.0 21.9 %transform.1 = f32[3,15552]{1,0:T(4,128)S(1)} custom-call(s32[1280]{0:T(1024)} %wave_hbm.1, s32[12]{0:T(128)} %lat_hbm.1, s32[6]{0:T(128)} %cycle_hbm.1, bf16[6,320,1280]{2,1,0:T(8,128)(2,1)} %bitcast.2, bf16[6,320,1280]{2,1,0:T(8,128)(2,1)} %bitcast.3), custom_call_target="tpu_custom_call" | custom-call | tf_op jit(solution)/shard_map/transform/pallas_call | solution.py:489
  21.9 0.7 %copy.7 = f32[3,15552]{1,0:T(4,128)} copy(f32[3,15552]{1,0:T(4,128)S(1)} %transform.1) | data formatting | bytes 373248

commit v6 on v5

--- a/solution.py
+++ b/solution.py
@@ -11,7 +11,7 @@
 RMAX = 5136
 LANES = 128
 BLOCK = 16
-AHEAD = 3
+AHEAD = 2
 
 
 def split(value):
@@ -248,7 +248,7 @@
         kept.start()
         wave_copies[1].append(kept)
 
-    early = min(2, cycles)
+    early = min(1, cycles)
     for r in range(early):
         for t in range(tiles):
             tables(r, t)
@@ -470,11 +470,11 @@
     fields = parts // 2
     cycles = lat_order.shape[0] // wave_count
     groups = (slot_count + LANES - 1) // LANES
-    chunks, left = [], slot_count
-    while left:
-        size = 64 if 64 < left < slot_count else min(left, 32)
-        chunks.append(size)
-        left -= size
+    edge = max(BLOCK, slot_count // 5 // BLOCK * BLOCK)
+    middle = max(0, slot_count - 2 * edge)
+    chunks = [edge, middle // 2 // BLOCK * BLOCK]
+    chunks += [middle - chunks[1], slot_count - edge - middle]
+    chunks = [size for size in chunks if size > 0]
     packed = 0 < slot_count % LANES <= LANES // 2
     half_rows = 2 * lev_count
     counts = (half_step + 15) // 16

time: 22.8 us -> 21.9 us (0.961)
  Pallas kernels: 21.9 us -> 21.1 us
    pallas_call x1, Pallas kernels: 21.9 us -> 21.1 us  [local(): pl.pallas_call(functools.partial(kernel, half_step, tuple(chunks)), out_s...]
where the time goes in v6:
time: 21.9 us; the launch traced here: 21.8 us
  Pallas kernels  21.1 us (96%)
  local copies, waits for them, and re-layouts  0.7 us (3%)
    pallas_call x1, Pallas kernels, local(): pl.pallas_call(functools.partial(kernel, half_step, tuple(chunks)), out_s...  21.1 us
    unnamed x1, local copies, waits for them, and re-layouts  0.7 us

profile of v6, /device:TPU:0, one launch (start us, length us, event | category | flops | bytes accessed | tf_op | source)
XLA Modules:
  0.0 21.8 jit_solution(12579901383881807624)
XLA Ops:
  0.0 21.1 %transform.1 = f32[3,15552]{1,0:T(4,128)S(1)} custom-call(s32[1280]{0:T(1024)} %wave_hbm.1, s32[12]{0:T(128)} %lat_hbm.1, s32[6]{0:T(128)} %cycle_hbm.1, bf16[6,320,1280]{2,1,0:T(8,128)(2,1)} %bitcast.2, bf16[6,320,1280]{2,1,0:T(8,128)(2,1)} %bitcast.3), custom_call_target="tpu_custom_call" | custom-call | tf_op jit(solution)/shard_map/transform/pallas_call | solution.py:489
  21.1 0.7 %copy.7 = f32[3,15552]{1,0:T(4,128)} copy(f32[3,15552]{1,0:T(4,128)S(1)} %transform.1) | data formatting | bytes 373248

commit v7 on v6

--- a/solution.py
+++ b/solution.py
@@ -264,6 +264,9 @@
     pending = None
     for b in range(total_blocks):
         if b * BLOCK in starts:
+            if pending is not None and b % turns_count == 0:
+                finish(*pending)
+                pending = None
             i = starts.index(b * BLOCK)
             for copy in loads[i]:
                 copy.wait()

time: 21.9 us -> 21.6 us (0.986)
  Pallas kernels: 21.1 us -> 20.8 us
    pallas_call x1, Pallas kernels: 21.1 us -> 20.8 us  [local(): pl.pallas_call(functools.partial(kernel, half_step, tuple(chunks)), out_s...]
where the time goes in v7:
time: 21.6 us; the launch traced here: 21.5 us
  Pallas kernels  20.8 us (96%)
  local copies, waits for them, and re-layouts  0.7 us (3%)
    pallas_call x1, Pallas kernels, local(): pl.pallas_call(functools.partial(kernel, half_step, tuple(chunks)), out_s...  20.8 us
    unnamed x1, local copies, waits for them, and re-layouts  0.7 us

profile of v7, /device:TPU:0, one launch (start us, length us, event | category | flops | bytes accessed | tf_op | source)
XLA Modules:
  0.0 21.5 jit_solution(2478417405843840953)
XLA Ops:
  0.0 20.8 %transform.1 = f32[3,15552]{1,0:T(4,128)S(1)} custom-call(s32[1280]{0:T(1024)} %wave_hbm.1, s32[12]{0:T(128)} %lat_hbm.1, s32[6]{0:T(128)} %cycle_hbm.1, bf16[6,320,1280]{2,1,0:T(8,128)(2,1)} %bitcast.2, bf16[6,320,1280]{2,1,0:T(8,128)(2,1)} %bitcast.3), custom_call_target="tpu_custom_call" | custom-call | tf_op jit(solution)/shard_map/transform/pallas_call | solution.py:492
  20.8 0.7 %copy.7 = f32[3,15552]{1,0:T(4,128)} copy(f32[3,15552]{1,0:T(4,128)S(1)} %transform.1) | data formatting | bytes 373248

commit v8 on v7

--- a/solution.py
+++ b/solution.py
@@ -364,13 +364,13 @@
     for copy in wave_copies[True]:
         copy.wait()
     if halves == 2:
-        begun = transform(0, 0)
+        begun = [transform(r, 0) for r in range(cycles)]
     for copy in wave_copies[False]:
         copy.wait()
 
     for r in range(cycles):
         if halves == 2:
-            first = begun if r == 0 else transform(r, 0)
+            first = begun[r]
             value = [one + two for one, two in zip(first, transform(r, 1))]
         else:
             value = transform(r, 0)

time: 21.6 us -> 21.4 us (level)
  no operation moved by 1% of the time
where the time goes in v8:
time: 21.4 us; the launch traced here: 21.3 us
  Pallas kernels  20.6 us (96%)
  local copies, waits for them, and re-layouts  0.7 us (3%)
    pallas_call x1, Pallas kernels, local(): pl.pallas_call(functools.partial(kernel, half_step, tuple(chunks)), out_s...  20.6 us
    unnamed x1, local copies, waits for them, and re-layouts  0.7 us

profile of v8, /device:TPU:0, one launch (start us, length us, event | category | flops | bytes accessed | tf_op | source)
XLA Modules:
  0.0 21.3 jit_solution(9713361816516062344)
XLA Ops:
  0.0 20.6 %transform.1 = f32[3,15552]{1,0:T(4,128)S(1)} custom-call(s32[1280]{0:T(1024)} %wave_hbm.1, s32[12]{0:T(128)} %lat_hbm.1, s32[6]{0:T(128)} %cycle_hbm.1, bf16[6,320,1280]{2,1,0:T(8,128)(2,1)} %bitcast.2, bf16[6,320,1280]{2,1,0:T(8,128)(2,1)} %bitcast.3), custom_call_target="tpu_custom_call" | custom-call | tf_op jit(solution)/shard_map/transform/pallas_call | solution.py:492
  20.6 0.7 %copy.7 = f32[3,15552]{1,0:T(4,128)} copy(f32[3,15552]{1,0:T(4,128)S(1)} %transform.1) | data formatting | bytes 373248
